TPU v7x, 32 devices: a whole 2x2x4 slice. The times are simulated.
32 devices in a mesh: lat: 8 (over z, x), lon: 4 (over y, core).
Axes of the slice: x: 2, y: 2, z: 4, core: 2. Of those that a mesh axis runs over, the one named last changes fastest.
Arguments:
- state: bfloat16 [32, 32, 64, 128], P('lat', 'lon'), may hold values from -6 to 6
- obs_row: int32 [32, 32, 128], P('lat', 'lon'), may hold values from 0 to 63
- obs_count: int32 [32, 32], P('lat', 'lon'), may hold values from 0 to 128
- obs_value: float32 [32, 32, 128], P('lat', 'lon'), may hold values from -6 to 6
- obs_weight: float32 [32, 32, 128], P('lat', 'lon'), may hold values from 0.5 to 2
- quadrant: int32 [32, 32, 64], P('lat', 'lon'), may hold values from 0 to 3
- frac_lat: float32 [32, 32, 64], P('lat', 'lon'), may hold values from 0 to 1
- frac_lon: float32 [32, 32, 64], P('lat', 'lon'), may hold values from 0 to 1
- land: int32 [32, 32, 64], P('lat', 'lon'), may hold values 0 or 1
Outputs:
- analysis: bfloat16 [32, 32, 64, 128], P('lat', 'lon')
All inputs are finite; a program needn't handle non-finite values. No bound on the sum of `land` on one device may be relied on, other than what follows from the above.
Results may differ from a plain program's by a relative error of at most 0.0051.
Values may be sent and summed in bfloat16 or wider, within the bound.
A program may use at most 64 MiB of HBM per device.

v0:
```python
import functools
import math

import jax
import jax.numpy as jnp
from jax import lax
from jax.experimental import pallas as pl
from jax.experimental.pallas import tpu as pltpu
from jax.sharding import PartitionSpec as P

ITERS = 6
NEAR = (0.5, 1.0, 0.5)
SIDE_ROWS = 8
F32 = jnp.float32
BF16 = jnp.bfloat16
MESH = pl.DeviceIdType.MESH
WAYS = ((-1, 0), (1, 0), (0, -1), (0, 1))
CORNERS = ((-1, -1), (-1, 1), (1, -1), (1, 1))


def nn(a, b):
    return lax.dot_general(a, b, (((1,), (0,)), ((), ())), preferred_element_type=F32)


def nt(a, b):
    return lax.dot_general(a, b, (((1,), (1,)), ((), ())), preferred_element_type=F32)


def tn(a, b):
    return lax.dot_general(a, b, (((0,), (0,)), ((), ())), preferred_element_type=F32)


def group_of(count, most=4):
    return next(g for g in range(most, 0, -1) if count % g == 0)


def prep_kernel(count_ref, state_ref, row_ref, value_ref, weight_ref, out_ref):
    tile_lat, tile_lon, cells, members = state_ref.shape
    slots = row_ref.shape[-1]
    nodes = tile_lat * tile_lon
    group = group_of(nodes, 8)

    def step(t, carry):
        for g in range(group):
            node = t * group + g
            i, j = node // tile_lon, node % tile_lon
            values = state_ref[i, j].astype(F32)
            mean = jnp.sum(values, axis=1, keepdims=True) * (1.0 / members)
            pert = values - mean
            lane = lax.broadcasted_iota(jnp.int32, (1, slots), 1)
            weight = jnp.where(lane < count_ref[i, j], weight_ref[i, pl.ds(j, 1), :], 0.0)
            square = weight * weight
            hit = row_ref[i, pl.ds(j, 1), :] == lax.broadcasted_iota(jnp.int32, (cells, slots), 0)
            density = jnp.sum(jnp.where(hit, square, 0.0), axis=1, keepdims=True)
            pulled = jnp.sum(
                jnp.where(hit, square * value_ref[i, pl.ds(j, 1), :], 0.0), axis=1, keepdims=True
            )
            out_ref[i, j, pl.ds(0, cells), :] = (jnp.sqrt(density) * pert).astype(BF16)
            side = jnp.sum(pert * (pulled - density * mean), axis=0, keepdims=True)
            high = side.astype(BF16).astype(F32)
            which = lax.broadcasted_iota(jnp.int32, (SIDE_ROWS, members), 0)
            tail = jnp.where(which == 0, high, jnp.where(which == 1, side - high, 0.0))
            out_ref[i, j, pl.ds(cells, SIDE_ROWS), :] = tail.astype(BF16)
        return carry

    lax.fori_loop(0, nodes // group, step, 0)


def edge_slices(step, size):
    if step == 0:
        return slice(0, size), slice(1, size + 1), size
    if step < 0:
        return 0, size + 1, 1
    return size - 1, 0, 1


def main_kernel(
    counts, qx_ref, state_ref, quadrant_ref, frac_lat_ref, frac_lon_ref, land_ref,
    out_ref, qbuf, wbuf, q_send, q_recv, w_send, w_recv, r_send, r_recv,
    c_send, c_recv,
):
    n_lat, n_lon = counts
    row_parts = r_send.shape[1]
    tile_lat, tile_lon, cells, members = state_ref.shape
    lat, lon = lax.axis_index("lat"), lax.axis_index("lon")

    def exists(way):
        if way[0] < 0:
            return lat > 0
        if way[0] > 0:
            return lat < n_lat - 1
        return None

    def where_exists(way, do):
        if way[0] == 0:
            do()
        else:
            pl.when(exists(way))(do)

    def peer(way):
        return (lat + way[0], lax.rem(lon + way[1] + n_lon, n_lon))

    def at(ref, i, j):
        i = pl.ds(i.start, i.stop - i.start) if isinstance(i, slice) else i
        j = pl.ds(j.start, j.stop - j.start) if isinstance(j, slice) else j
        return ref.at[i, j]

    def copy(source, offset, buffer, send, recv, index):
        way = WAYS[index]
        si, di, _ = edge_slices(way[0], tile_lat)
        sj, dj, _ = edge_slices(way[1], tile_lon)

        def moved(s):
            return slice(s.start + offset, s.stop + offset) if isinstance(s, slice) else s + offset

        return pltpu.make_async_remote_copy(
            src_ref=at(source, moved(si), moved(sj)),
            dst_ref=at(buffer, di, dj),
            send_sem=send.at[index],
            recv_sem=recv.at[index],
            device_id=peer(way),
            device_id_type=MESH,
        )

    def q_copy(index):
        return copy(qx_ref, 0, qbuf, q_send, q_recv, index)

    def w_copy(index):
        return copy(wbuf, 1, wbuf, w_send, w_recv, index)

    def row_copy(index, part):
        source, target, _ = edge_slices(WAYS[index][0], tile_lat)
        width = tile_lon // row_parts
        columns = pl.ds(1 + part * width, width)
        return pltpu.make_async_remote_copy(
            src_ref=wbuf.at[source + 1, columns],
            dst_ref=wbuf.at[target, columns],
            send_sem=r_send.at[index, part],
            recv_sem=r_recv.at[index, part],
            device_id=peer(WAYS[index]),
            device_id_type=MESH,
        )

    def corner_copy(buffer, stage, index):
        side, step = CORNERS[index]
        row = 0 if side < 0 else tile_lat + 1
        source, target = (1, tile_lon + 1) if step < 0 else (tile_lon, 0)
        return pltpu.make_async_remote_copy(
            src_ref=buffer.at[row, source],
            dst_ref=buffer.at[row, target],
            send_sem=c_send.at[stage, index],
            recv_sem=c_recv.at[stage, index],
            device_id=peer((0, step)),
            device_id_type=MESH,
        )

    def each_corner(buffer, stage, do):
        for index, way in enumerate(CORNERS):
            where_exists(way, lambda index=index: do(corner_copy(buffer, stage, index)))

    barrier = pltpu.get_barrier_semaphore()
    for way in WAYS:
        where_exists(way, lambda way=way: pl.semaphore_signal(
            barrier, inc=1, device_id=peer(way), device_id_type=MESH))
    present = 2 + (lat > 0).astype(jnp.int32) + (lat < n_lat - 1).astype(jnp.int32)
    pl.semaphore_wait(barrier, present)
    for index, way in enumerate(WAYS):
        where_exists(way, lambda index=index: q_copy(index).start())

    @pl.when(lat == 0)
    def _():
        qbuf[0] = jnp.zeros(qbuf.shape[1:], BF16)
        wbuf[0] = jnp.zeros(wbuf.shape[1:], BF16)

    @pl.when(lat == n_lat - 1)
    def _():
        qbuf[tile_lat + 1] = jnp.zeros(qbuf.shape[1:], BF16)
        wbuf[tile_lat + 1] = jnp.zeros(wbuf.shape[1:], BF16)

    for i in range(tile_lat):
        qbuf[i + 1, pl.ds(1, tile_lon)] = qx_ref[i]

    def received(index, make):
        way = WAYS[index]
        back = (-way[0], -way[1])
        where_exists(back, lambda: make(index).wait_recv())

    def sent(index, make):
        where_exists(WAYS[index], lambda: make(index).wait_send())

    eye = (
        lax.broadcasted_iota(jnp.int32, (members, members), 0)
        == lax.broadcasted_iota(jnp.int32, (members, members), 1)
    ).astype(F32)
    eye_b = eye.astype(BF16)

    def gram_of(i, j):
        left, right = [], []
        tail = jnp.zeros((SIDE_ROWS, members), F32)
        for b in range(3):
            for a in range(3):
                scale = NEAR[a] * NEAR[b]
                block = qbuf[i + a, j + b, pl.ds(0, cells), :]
                right.append(block)
                left.append(block if scale == 1.0 else block * jnp.asarray(scale, BF16))
                tail += scale * qbuf[i + a, j + b, pl.ds(cells, SIDE_ROWS), :].astype(F32)
        gram = tn(jnp.concatenate(left, axis=0), jnp.concatenate(right, axis=0))
        return gram, jnp.sum(tail, axis=0, keepdims=True)

    def total(x):
        return jnp.sum(jnp.sum(x, axis=0, keepdims=True), axis=1, keepdims=True)

    def transform(places):
        group = range(len(places))
        terms = [gram_of(i, j) for i, j in places]
        frobs, cy, ey, cz, ez = [], [], [], [], []
        for gram, _ in terms:
            ridge = members - 1.0
            trace = total(gram * eye)
            frob = jnp.sqrt(total(gram * gram) + 2.0 * ridge * trace + ridge * ridge * members)
            centre = ridge + trace * (1.0 / members)
            inv = 1.0 / centre
            rest = gram * inv + eye * (ridge * inv - 1.0)
            frobs.append(frob)
            start = centre / frob
            cf = 1.5 - 0.5 * start
            ef = rest * (-0.5 * start / cf)
            cy.append(cf * start)
            ey.append((ef + rest) + nn(ef.astype(BF16), rest.astype(BF16)))
            cz.append(cf)
            ez.append(ef)
        for step in range(1, ITERS):
            last = step == ITERS - 1
            ybs = [e.astype(BF16) for e in ey]
            zbs = [e.astype(BF16) for e in ez]
            prods = [nn(zb, yb) for zb, yb in zip(zbs, ybs)]
            cts = [y * z for y, z in zip(cy, cz)]
            cfs = [1.5 - 0.5 * ct for ct in cts]
            efs = [
                ((ey[n] + ez[n]) + prods[n]) * (-0.5 * cts[n] / cfs[n]) for n in group
            ]
            fbs = [e.astype(BF16) for e in efs]
            if last:
                both = [nn(fb, zb) for fb, zb in zip(fbs, zbs)]
            else:
                both = [
                    nn(fb, jnp.concatenate([zb, yb], axis=1))
                    for fb, zb, yb in zip(fbs, zbs, ybs)
                ]
            for n in group:
                if not last:
                    ey[n] = (efs[n] + ey[n]) + both[n][:, members:]
                    cy[n] = cfs[n] * cy[n]
                ez[n] = (efs[n] + ez[n]) + both[n][:, :members]
                cz[n] = cfs[n] * cz[n]
        which = lax.broadcasted_iota(jnp.int32, (SIDE_ROWS, members), 0)
        for n, (i, j) in enumerate(places):
            side = terms[n][1]
            zb = ez[n].astype(BF16)
            high = side.astype(BF16).astype(F32)
            rows = jnp.where(which == 0, high, jnp.where(which == 1, side - high, 0.0))
            inner = side + jnp.sum(nn(rows.astype(BF16), zb), axis=0, keepdims=True)
            inner = inner * (cz[n] * cz[n] / frobs[n])
            high = inner.astype(BF16)
            low = (inner - high.astype(F32)).astype(BF16)
            high = jnp.broadcast_to(high, (members, members))
            low = jnp.broadcast_to(low, (members, members))
            mean_weight = nt(
                jnp.concatenate([zb, eye_b, eye_b], axis=1),
                jnp.concatenate([high, high, low], axis=1),
            )
            spread = math.sqrt(members - 1) * cz[n] / jnp.sqrt(frobs[n])
            wbuf[i + 1, j + 1] = (mean_weight + spread * (ez[n] + eye)).astype(BF16)

    mid_lat, mid_lon = tile_lat - 2, tile_lon - 2
    n_rows, n_sides, n_inner = 2 * tile_lon, 2 * mid_lat, mid_lat * mid_lon
    group = n_rows // row_parts
    ahead = n_inner // group
    g_rows, g_sides, g_inner = n_rows // group, n_sides // group, n_inner // group

    def row_place(k):
        return (k % 2) * (tile_lat - 1), k // 2

    def side_place(k):
        return 1 + k // 2, (k % 2) * (tile_lon - 1)

    def inner_place(k):
        return 1 + k // mid_lon, 1 + k % mid_lon

    def place(slot, g):
        rows = slot - ahead
        sides = rows - g_rows
        after = slot - g_rows - g_sides
        is_inner = (slot < ahead) | (sides >= g_sides)
        inner = inner_place(jnp.where(slot < ahead, slot, jnp.maximum(after, 0)) * group + g)
        row = row_place(jnp.clip(rows, 0, g_rows - 1) * group + g)
        side = side_place(jnp.clip(sides, 0, g_sides - 1) * group + g)
        i = jnp.where(is_inner, inner[0], jnp.where(sides >= 0, side[0], row[0]))
        j = jnp.where(is_inner, inner[1], jnp.where(sides >= 0, side[1], row[1]))
        return i, j

    def node_step(slot, carry):
        @pl.when(slot == ahead - 1)
        def _():
            for index in range(2):
                received(index, q_copy)
            each_corner(qbuf, 0, lambda copy: copy.start())

        @pl.when(slot == ahead)
        def _():
            for index in range(2, 4):
                received(index, q_copy)
            each_corner(qbuf, 0, lambda copy: copy.wait_recv())

        transform([place(slot, g) for g in range(group)])

        for index in range(2):
            part = slot - ahead
            pl.when(exists(WAYS[index]) & (part >= 0) & (part < g_rows))(
                lambda index=index, part=part: row_copy(index, part).start())

        @pl.when(slot == ahead + g_rows + g_sides - 1)
        def _():
            for index in range(2, 4):
                w_copy(index).start()

        return carry

    lax.fori_loop(0, g_rows + g_sides + g_inner, node_step, 0)

    def analyse(i, j):
        values = state_ref[i, j].astype(F32)
        mean = jnp.sum(values, axis=1, keepdims=True) * (1.0 / members)
        pert = (values - mean).astype(BF16)
        corner = quadrant_ref[i, pl.ds(j, 1), :]
        along = []
        for half, frac in (
            (corner // 2, frac_lat_ref[i, pl.ds(j, 1), :]),
            (corner % 2, frac_lon_ref[i, pl.ds(j, 1), :]),
        ):
            for a in range(3):
                along.append(
                    jnp.where(half == a, 1.0 - frac, 0.0) + jnp.where(half + 1 == a, frac, 0.0)
                )
        along.append(land_ref[i, pl.ds(j, 1), :].astype(F32))
        along.append(jnp.zeros_like(along[0]))
        coef = jnp.transpose(jnp.concatenate(along, axis=0))
        acc = mean
        for a in range(3):
            wide = jnp.concatenate([wbuf[i + a, j + b] for b in range(3)], axis=1)
            prod = nn(pert, wide)
            row = sum(
                coef[:, 3 + b : 4 + b] * prod[:, b * members : (b + 1) * members] for b in range(3)
            )
            acc = acc + coef[:, a : a + 1] * row
        result = jnp.where(coef[:, 6:7] == 1.0, acc, values)
        out_ref[i, j] = result.astype(BF16)

    def inner_step(t, carry):
        for g in range(group):
            analyse(*inner_place(t * group + g))
        return carry

    lax.fori_loop(0, g_inner, inner_step, 0)
    for index in range(2):
        for part in range(row_parts):
            received(index, lambda index, part=part: row_copy(index, part))
    each_corner(wbuf, 1, lambda copy: copy.start())
    for index in range(2, len(WAYS)):
        received(index, w_copy)

    def rim_step(t, carry):
        @pl.when(t == g_sides + row_parts - 2)
        def _():
            each_corner(wbuf, 1, lambda copy: copy.wait_recv())

        part = lax.rem(t - g_sides + 1 + row_parts, row_parts)
        first = jnp.where(t < g_sides, n_rows + t * group, part * group)
        for g in range(group):
            k = first + g
            row, side = row_place(jnp.minimum(k, n_rows - 1)), side_place(jnp.maximum(k - n_rows, 0))
            analyse(jnp.where(k < n_rows, row[0], side[0]), jnp.where(k < n_rows, row[1], side[1]))
        return carry

    lax.fori_loop(0, g_rows + g_sides, rim_step, 0)
    for index in range(len(WAYS)):
        sent(index, q_copy)
        if index >= 2:
            sent(index, w_copy)
        else:
            for part in range(row_parts):
                sent(index, lambda index, part=part: row_copy(index, part))
    each_corner(qbuf, 0, lambda copy: copy.wait_send())
    each_corner(wbuf, 1, lambda copy: copy.wait_send())


VM = pl.BlockSpec(memory_space=pltpu.VMEM)


def body(counts, state, obs_row, obs_count, obs_value, obs_weight, quadrant, frac_lat, frac_lon, land):
    tile_lat, tile_lon, cells, members = state.shape
    rows = cells + SIDE_ROWS
    sizes = (2 * tile_lon, 2 * (tile_lat - 2), (tile_lat - 2) * (tile_lon - 2))
    row_parts = 2 * tile_lon // next(g for g in (4, 2) if all(n % g == 0 for n in sizes))
    qx = pl.pallas_call(
        prep_kernel,
        out_shape=jax.ShapeDtypeStruct((tile_lat, tile_lon, rows, members), BF16),
        in_specs=[pl.BlockSpec(memory_space=pltpu.SMEM)] + [VM] * 4,
        out_specs=VM,
        name="prep",
    )(obs_count, state, obs_row, obs_value, obs_weight)
    return pl.pallas_call(
        functools.partial(main_kernel, counts),
        out_shape=jax.ShapeDtypeStruct(state.shape, BF16),
        in_specs=[VM] * 6,
        out_specs=VM,
        scratch_shapes=[
            pltpu.VMEM((tile_lat + 2, tile_lon + 2, rows, members), BF16),
            pltpu.VMEM((tile_lat + 2, tile_lon + 2, members, members), BF16),
            pltpu.SemaphoreType.DMA((4,)),
            pltpu.SemaphoreType.DMA((4,)),
            pltpu.SemaphoreType.DMA((4,)),
            pltpu.SemaphoreType.DMA((4,)),
            pltpu.SemaphoreType.DMA((2, row_parts)),
            pltpu.SemaphoreType.DMA((2, row_parts)),
            pltpu.SemaphoreType.DMA((2, 4)),
            pltpu.SemaphoreType.DMA((2, 4)),
        ],
        compiler_params=pltpu.CompilerParams(
            collective_id=0, has_side_effects=True, vmem_limit_bytes=48 * 1024 * 1024
        ),
        name="analyse",
    )(qx, state, quadrant, frac_lat, frac_lon, land)


def solution(mesh):
    counts = (mesh.shape["lat"], mesh.shape["lon"])
    return jax.shard_map(
        functools.partial(body, counts),
        mesh=mesh,
        in_specs=(
            P("lat", "lon", None, None),
            P("lat", "lon", None),
            P("lat", "lon"),
            P("lat", "lon", None),
            P("lat", "lon", None),
            P("lat", "lon", None),
            P("lat", "lon", None),
            P("lat", "lon", None),
            P("lat", "lon", None),
        ),
        out_specs=P("lat", "lon", None, None),
        check_vma=False,
    )
```

profile of v0, /device:TPU:17, one launch (start us, length us, event | category | flops | bytes accessed | tf_op | source)
XLA Modules:
  0.0 42.3 jit_solution(11487896579387010698)
XLA Ops:
  0.0 0.0 copy-start.1
  0.0 0.0 copy-start.5
  0.0 0.0 copy-start.4
  0.0 0.0 copy-start.3
  0.0 0.0 copy-start.2
  0.0 3.2 %prep.1.qx_ref = bf16[4,8,72,128]{3,2,1,0:T(8,128)(2,1)} custom-call(s32[4,8]{1,0:T(4,128)} %count_ref.1, bf16[4,8,64,128]{3,2,1,0:T(8,128)(2,1)} %state_ref.3, s32[4,8,128]{2,1,0:T(8,128)} %row_ref.1, f32[4,8,128]{2,1,0:T(8,128)} %value_ref.1, f32[4,8,128]{2,1,0:T(8,128)} %weight_ref.1), custom_call_target="tpu_custom_call" | custom-call | tf_op jit(solution)/shard_map/prep/pallas_call | solution.py:405
  3.2 0.0 copy-done.1
  3.2 0.0 copy-done.5
  3.2 0.0 copy-done.4
  3.2 0.0 copy-done.3
  3.2 0.0 copy-done.2
  3.2 0.0 copy-start
  3.2 1.1 %copy-done = bf16[4,8,72,128]{3,2,1,0:T(8,128)(2,1)S(1)} copy-done((bf16[4,8,72,128]{3,2,1,0:T(8,128)(2,1)S(1)}, bf16[4,8,72,128]{3,2,1,0:T(8,128)(2,1)}, u32[]{:S(2)}) %copy-start) | copy-done | bytes 589848
  4.3 37.2 %analyse.1 = bf16[4,8,64,128]{3,2,1,0:T(8,128)(2,1)S(1)} custom-call(bf16[4,8,72,128]{3,2,1,0:T(8,128)(2,1)S(1)} %copy-done, bf16[4,8,64,128]{3,2,1,0:T(8,128)(2,1)S(1)} %copy-done.1, s32[4,8,64]{2,1,0:T(8,128)S(1)} %copy-done.2, f32[4,8,64]{2,1,0:T(8,128)S(1)} %copy-done.3, f32[4,8,64]{2,1,0:T(8,128)S(1)} %copy-done.4, s32[4,8,64]{2,1,0:T(8,128)S(1)} %copy-done.5), custom_call_target="tpu_custom_call" | custom-call | tf_op jit(solution)/shard_map/analyse/pallas_call | solution.py:412
  41.5 0.8 %copy.11 = bf16[4,8,64,128]{3,2,1,0:T(8,128)(2,1)} copy(bf16[4,8,64,128]{3,2,1,0:T(8,128)(2,1)S(1)} %analyse.1) | data formatting | bytes 1048576
Async XLA Ops:
  0.0 3.2 %copy-start.1 = (bf16[4,8,64,128]{3,2,1,0:T(8,128)(2,1)S(1)}, bf16[4,8,64,128]{3,2,1,0:T(8,128)(2,1)}, u32[]{:S(2)}) copy-start(bf16[4,8,64,128]{3,2,1,0:T(8,128)(2,1)} %state_ref.3) | copy-start | bytes 1572868
  0.0 3.2 %copy-start.5 = (s32[4,8,64]{2,1,0:T(8,128)S(1)}, s32[4,8,64]{2,1,0:T(8,128)}, u32[]{:S(2)}) copy-start(s32[4,8,64]{2,1,0:T(8,128)} %land_ref.1) | copy-start | bytes 24580
  0.0 3.2 %copy-start.4 = (f32[4,8,64]{2,1,0:T(8,128)S(1)}, f32[4,8,64]{2,1,0:T(8,128)}, u32[]{:S(2)}) copy-start(f32[4,8,64]{2,1,0:T(8,128)} %frac_lon_ref.1) | copy-start | bytes 24580
  0.0 3.2 %copy-start.3 = (f32[4,8,64]{2,1,0:T(8,128)S(1)}, f32[4,8,64]{2,1,0:T(8,128)}, u32[]{:S(2)}) copy-start(f32[4,8,64]{2,1,0:T(8,128)} %frac_lat_ref.1) | copy-start | bytes 24580
  0.0 3.2 %copy-start.2 = (s32[4,8,64]{2,1,0:T(8,128)S(1)}, s32[4,8,64]{2,1,0:T(8,128)}, u32[]{:S(2)}) copy-start(s32[4,8,64]{2,1,0:T(8,128)} %quadrant_ref.1) | copy-start | bytes 24580
  3.2 1.1 %copy-start = (bf16[4,8,72,128]{3,2,1,0:T(8,128)(2,1)S(1)}, bf16[4,8,72,128]{3,2,1,0:T(8,128)(2,1)}, u32[]{:S(2)}) copy-start(bf16[4,8,72,128]{3,2,1,0:T(8,128)(2,1)} %prep.1.qx_ref) | copy-start | bytes 1769476
where the time goes:
time: 42.5 us; the launch traced here: 42.3 us
  Pallas kernels  40.4 us (95%)
  local copies, waits for them, and re-layouts  1.87 us (4%)
    pallas_call x1, Pallas kernels, body(): pl.pallas_call(functools.partial(main_kernel, counts), out_shape=jax.Shap...  37.2 us
    pallas_call x1, Pallas kernels, body(): pl.pallas_call(prep_kernel, out_shape=jax.ShapeDtypeStruct((tile_lat, til...  3.17 us
    unnamed x13, local copies, waits for them, and re-layouts  1.87 us

commit v1 on v0

--- a/solution.py
+++ b/solution.py
@@ -210,57 +210,65 @@
     def total(x):
         return jnp.sum(jnp.sum(x, axis=0, keepdims=True), axis=1, keepdims=True)
 
+    def pair_factor(scale):
+        first = 1.5 - 0.5 * scale
+        r = 0.5 * scale / first
+        middle = scale * first * first
+        second = 1.5 - 0.5 * middle
+        q = 0.5 * middle / second
+        p1, p2, p3 = 1.0 - 2.0 * r, r * r - 2.0 * r, r * r
+        coefs = (-r - q * p1, q * (r * p1 - p2), q * (r * p2 - p3), q * r * p3)
+        both = first * second
+        return both, coefs, scale * both * both
+
     def transform(places):
         group = range(len(places))
-        terms = [gram_of(i, j) for i, j in places]
-        frobs, cy, ey, cz, ez = [], [], [], [], []
-        for gram, _ in terms:
+        xs, sides, scalars = [], [], []
+        for i, j in places:
+            gram, side = gram_of(i, j)
             ridge = members - 1.0
             trace = total(gram * eye)
             frob = jnp.sqrt(total(gram * gram) + 2.0 * ridge * trace + ridge * ridge * members)
             centre = ridge + trace * (1.0 / members)
             inv = 1.0 / centre
-            rest = gram * inv + eye * (ridge * inv - 1.0)
-            frobs.append(frob)
-            start = centre / frob
-            cf = 1.5 - 0.5 * start
-            ef = rest * (-0.5 * start / cf)
-            cy.append(cf * start)
-            ey.append((ef + rest) + nn(ef.astype(BF16), rest.astype(BF16)))
-            cz.append(cf)
-            ez.append(ef)
-        for step in range(1, ITERS):
-            last = step == ITERS - 1
-            ybs = [e.astype(BF16) for e in ey]
-            zbs = [e.astype(BF16) for e in ez]
-            prods = [nn(zb, yb) for zb, yb in zip(zbs, ybs)]
-            cts = [y * z for y, z in zip(cy, cz)]
-            cfs = [1.5 - 0.5 * ct for ct in cts]
-            efs = [
-                ((ey[n] + ez[n]) + prods[n]) * (-0.5 * cts[n] / cfs[n]) for n in group
-            ]
-            fbs = [e.astype(BF16) for e in efs]
-            if last:
-                both = [nn(fb, zb) for fb, zb in zip(fbs, zbs)]
-            else:
-                both = [
-                    nn(fb, jnp.concatenate([zb, yb], axis=1))
-                    for fb, zb, yb in zip(fbs, zbs, ybs)
-                ]
+            xs.append(gram * inv + eye * (ridge * inv - 1.0))
+            sides.append(side)
+            scale = centre / frob
+            root, steps = 1.0, []
+            for _ in range(ITERS // 2):
+                both, coefs, scale = pair_factor(scale)
+                root = root * both
+                steps.append(coefs)
+            scalars.append((frob, root, steps))
+        zs = [None for _ in group]
+        for step in range(ITERS // 2):
+            last = step == ITERS // 2 - 1
+            squares, ds, gs = [], [], []
+            for x in xs:
+                xb = x.astype(BF16)
+                squares.append(nn(xb, xb))
             for n in group:
+                a1, a2, a3, a4 = scalars[n][2][step]
+                x, s = xs[n], squares[n]
+                tail = nn(s.astype(BF16), (a3 * x + a4 * s).astype(BF16))
+                ds.append(a1 * x + a2 * s + tail)
+            for n in group:
+                d = ds[n]
+                db = d.astype(BF16)
                 if not last:
-                    ey[n] = (efs[n] + ey[n]) + both[n][:, members:]
-                    cy[n] = cfs[n] * cy[n]
-                ez[n] = (efs[n] + ez[n]) + both[n][:, :members]
-                cz[n] = cfs[n] * cz[n]
+                    gs.append((xs[n] + d) + nn(db, xs[n].astype(BF16)))
+                zs[n] = d if step == 0 else (zs[n] + d) + nn(db, zs[n].astype(BF16))
+            if not last:
+                xs = [(gs[n] + ds[n]) + nn(ds[n].astype(BF16), gs[n].astype(BF16)) for n in group]
         which = lax.broadcasted_iota(jnp.int32, (SIDE_ROWS, members), 0)
         for n, (i, j) in enumerate(places):
-            side = terms[n][1]
-            zb = ez[n].astype(BF16)
+            frob, root, _ = scalars[n]
+            side = sides[n]
+            zb = zs[n].astype(BF16)
             high = side.astype(BF16).astype(F32)
             rows = jnp.where(which == 0, high, jnp.where(which == 1, side - high, 0.0))
             inner = side + jnp.sum(nn(rows.astype(BF16), zb), axis=0, keepdims=True)
-            inner = inner * (cz[n] * cz[n] / frobs[n])
+            inner = inner * (root * root / frob)
             high = inner.astype(BF16)
             low = (inner - high.astype(F32)).astype(BF16)
             high = jnp.broadcast_to(high, (members, members))
@@ -269,14 +277,15 @@
                 jnp.concatenate([zb, eye_b, eye_b], axis=1),
                 jnp.concatenate([high, high, low], axis=1),
             )
-            spread = math.sqrt(members - 1) * cz[n] / jnp.sqrt(frobs[n])
-            wbuf[i + 1, j + 1] = (mean_weight + spread * (ez[n] + eye)).astype(BF16)
+            spread = math.sqrt(members - 1) * root / jnp.sqrt(frob)
+            wbuf[i + 1, j + 1] = (mean_weight + spread * (zs[n] + eye)).astype(BF16)
 
     mid_lat, mid_lon = tile_lat - 2, tile_lon - 2
     n_rows, n_sides, n_inner = 2 * tile_lon, 2 * mid_lat, mid_lat * mid_lon
-    group = n_rows // row_parts
-    ahead = n_inner // group
+    group = next(g for g in (4, 2) if all(n % g == 0 for n in (n_rows, n_sides, n_inner)))
     g_rows, g_sides, g_inner = n_rows // group, n_sides // group, n_inner // group
+    wide = next(g for g in range(16, 0, -1) if n_rows % g == 0 and mid_lat * tile_lon % g == 0)
+    w_rows, w_rest = n_rows // wide, mid_lat * tile_lon // wide
 
     def row_place(k):
         return (k % 2) * (tile_lat - 1), k // 2
@@ -288,45 +297,30 @@
         return 1 + k // mid_lon, 1 + k % mid_lon
 
     def place(slot, g):
-        rows = slot - ahead
-        sides = rows - g_rows
-        after = slot - g_rows - g_sides
-        is_inner = (slot < ahead) | (sides >= g_sides)
-        inner = inner_place(jnp.where(slot < ahead, slot, jnp.maximum(after, 0)) * group + g)
-        row = row_place(jnp.clip(rows, 0, g_rows - 1) * group + g)
-        side = side_place(jnp.clip(sides, 0, g_sides - 1) * group + g)
-        i = jnp.where(is_inner, inner[0], jnp.where(sides >= 0, side[0], row[0]))
-        j = jnp.where(is_inner, inner[1], jnp.where(sides >= 0, side[1], row[1]))
-        return i, j
+        row = row_place(jnp.minimum(slot, w_rows - 1) * wide + g)
+        k = jnp.maximum(slot - w_rows, 0) * wide + g
+        rest = 1 + k // tile_lon, k % tile_lon
+        is_row = slot < w_rows
+        return jnp.where(is_row, row[0], rest[0]), jnp.where(is_row, row[1], rest[1])
+
+    for index in range(2):
+        received(index, q_copy)
+    each_corner(qbuf, 0, lambda copy: copy.start())
+    for index in range(2, 4):
+        received(index, q_copy)
+    each_corner(qbuf, 0, lambda copy: copy.wait_recv())
 
     def node_step(slot, carry):
-        @pl.when(slot == ahead - 1)
-        def _():
-            for index in range(2):
-                received(index, q_copy)
-            each_corner(qbuf, 0, lambda copy: copy.start())
-
-        @pl.when(slot == ahead)
-        def _():
-            for index in range(2, 4):
-                received(index, q_copy)
-            each_corner(qbuf, 0, lambda copy: copy.wait_recv())
-
-        transform([place(slot, g) for g in range(group)])
+        transform([place(slot, g) for g in range(wide)])
 
         for index in range(2):
-            part = slot - ahead
-            pl.when(exists(WAYS[index]) & (part >= 0) & (part < g_rows))(
-                lambda index=index, part=part: row_copy(index, part).start())
-
-        @pl.when(slot == ahead + g_rows + g_sides - 1)
-        def _():
-            for index in range(2, 4):
-                w_copy(index).start()
-
+            pl.when(exists(WAYS[index]) & (slot == w_rows - 1))(
+                lambda index=index: row_copy(index, 0).start())
         return carry
 
-    lax.fori_loop(0, g_rows + g_sides + g_inner, node_step, 0)
+    lax.fori_loop(0, w_rows + w_rest, node_step, 0)
+    for index in range(2, 4):
+        w_copy(index).start()
 
     def analyse(i, j):
         values = state_ref[i, j].astype(F32)
@@ -370,11 +364,11 @@
         received(index, w_copy)
 
     def rim_step(t, carry):
-        @pl.when(t == g_sides + row_parts - 2)
+        @pl.when(t == g_sides + g_rows - 2)
         def _():
             each_corner(wbuf, 1, lambda copy: copy.wait_recv())
 
-        part = lax.rem(t - g_sides + 1 + row_parts, row_parts)
+        part = lax.rem(t - g_sides + 1 + g_rows, g_rows)
         first = jnp.where(t < g_sides, n_rows + t * group, part * group)
         for g in range(group):
             k = first + g
@@ -400,8 +394,7 @@
 def body(counts, state, obs_row, obs_count, obs_value, obs_weight, quadrant, frac_lat, frac_lon, land):
     tile_lat, tile_lon, cells, members = state.shape
     rows = cells + SIDE_ROWS
-    sizes = (2 * tile_lon, 2 * (tile_lat - 2), (tile_lat - 2) * (tile_lon - 2))
-    row_parts = 2 * tile_lon // next(g for g in (4, 2) if all(n % g == 0 for n in sizes))
+    row_parts = 1
     qx = pl.pallas_call(
         prep_kernel,
         out_shape=jax.ShapeDtypeStruct((tile_lat, tile_lon, rows, members), BF16),

time: 42.5 us -> 42.9 us (level)
  no operation moved by 1% of the time
where the time goes in v1:
time: 42.9 us; the launch traced here: 42.5 us
  Pallas kernels  40.6 us (95%)
  local copies, waits for them, and re-layouts  1.87 us (4%)
    pallas_call x1, Pallas kernels, body(): pl.pallas_call(functools.partial(main_kernel, counts), out_shape=jax.Shap...  37.4 us
    pallas_call x1, Pallas kernels, body(): pl.pallas_call(prep_kernel, out_shape=jax.ShapeDtypeStruct((tile_lat, til...  3.17 us
    unnamed x13, local copies, waits for them, and re-layouts  1.87 us

profile of v1, /device:TPU:17, one launch (start us, length us, event | category | flops | bytes accessed | tf_op | source)
XLA Modules:
  0.0 42.5 jit_solution(8256267995818217481)
XLA Ops:
  0.0 0.0 copy-start.1
  0.0 0.0 copy-start.5
  0.0 0.0 copy-start.4
  0.0 0.0 copy-start.3
  0.0 0.0 copy-start.2
  0.0 3.2 %prep.1.qx_ref = bf16[4,8,72,128]{3,2,1,0:T(8,128)(2,1)} custom-call(s32[4,8]{1,0:T(4,128)} %count_ref.1, bf16[4,8,64,128]{3,2,1,0:T(8,128)(2,1)} %state_ref.3, s32[4,8,128]{2,1,0:T(8,128)} %row_ref.1, f32[4,8,128]{2,1,0:T(8,128)} %value_ref.1, f32[4,8,128]{2,1,0:T(8,128)} %weight_ref.1), custom_call_target="tpu_custom_call" | custom-call | tf_op jit(solution)/shard_map/prep/pallas_call | solution.py:398
  3.2 0.0 copy-done.1
  3.2 0.0 copy-done.5
  3.2 0.0 copy-done.4
  3.2 0.0 copy-done.3
  3.2 0.0 copy-done.2
  3.2 0.0 copy-start
  3.2 1.1 %copy-done = bf16[4,8,72,128]{3,2,1,0:T(8,128)(2,1)S(1)} copy-done((bf16[4,8,72,128]{3,2,1,0:T(8,128)(2,1)S(1)}, bf16[4,8,72,128]{3,2,1,0:T(8,128)(2,1)}, u32[]{:S(2)}) %copy-start) | copy-done | bytes 589848
  4.3 37.4 %analyse.1 = bf16[4,8,64,128]{3,2,1,0:T(8,128)(2,1)S(1)} custom-call(bf16[4,8,72,128]{3,2,1,0:T(8,128)(2,1)S(1)} %copy-done, bf16[4,8,64,128]{3,2,1,0:T(8,128)(2,1)S(1)} %copy-done.1, s32[4,8,64]{2,1,0:T(8,128)S(1)} %copy-done.2, f32[4,8,64]{2,1,0:T(8,128)S(1)} %copy-done.3, f32[4,8,64]{2,1,0:T(8,128)S(1)} %copy-done.4, s32[4,8,64]{2,1,0:T(8,128)S(1)} %copy-done.5), custom_call_target="tpu_custom_call" | custom-call | tf_op jit(solution)/shard_map/analyse/pallas_call | solution.py:405
  41.7 0.8 %copy.11 = bf16[4,8,64,128]{3,2,1,0:T(8,128)(2,1)} copy(bf16[4,8,64,128]{3,2,1,0:T(8,128)(2,1)S(1)} %analyse.1) | data formatting | bytes 1048576
Async XLA Ops:
  0.0 3.2 %copy-start.1 = (bf16[4,8,64,128]{3,2,1,0:T(8,128)(2,1)S(1)}, bf16[4,8,64,128]{3,2,1,0:T(8,128)(2,1)}, u32[]{:S(2)}) copy-start(bf16[4,8,64,128]{3,2,1,0:T(8,128)(2,1)} %state_ref.3) | copy-start | bytes 1572868
  0.0 3.2 %copy-start.5 = (s32[4,8,64]{2,1,0:T(8,128)S(1)}, s32[4,8,64]{2,1,0:T(8,128)}, u32[]{:S(2)}) copy-start(s32[4,8,64]{2,1,0:T(8,128)} %land_ref.1) | copy-start | bytes 24580
  0.0 3.2 %copy-start.4 = (f32[4,8,64]{2,1,0:T(8,128)S(1)}, f32[4,8,64]{2,1,0:T(8,128)}, u32[]{:S(2)}) copy-start(f32[4,8,64]{2,1,0:T(8,128)} %frac_lon_ref.1) | copy-start | bytes 24580
  0.0 3.2 %copy-start.3 = (f32[4,8,64]{2,1,0:T(8,128)S(1)}, f32[4,8,64]{2,1,0:T(8,128)}, u32[]{:S(2)}) copy-start(f32[4,8,64]{2,1,0:T(8,128)} %frac_lat_ref.1) | copy-start | bytes 24580
  0.0 3.2 %copy-start.2 = (s32[4,8,64]{2,1,0:T(8,128)S(1)}, s32[4,8,64]{2,1,0:T(8,128)}, u32[]{:S(2)}) copy-start(s32[4,8,64]{2,1,0:T(8,128)} %quadrant_ref.1) | copy-start | bytes 24580
  3.2 1.1 %copy-start = (bf16[4,8,72,128]{3,2,1,0:T(8,128)(2,1)S(1)}, bf16[4,8,72,128]{3,2,1,0:T(8,128)(2,1)}, u32[]{:S(2)}) copy-start(bf16[4,8,72,128]{3,2,1,0:T(8,128)(2,1)} %prep.1.qx_ref) | copy-start | bytes 1769476

commit v2 on v1

--- a/solution.py
+++ b/solution.py
@@ -76,7 +76,7 @@
 
 def main_kernel(
     counts, qx_ref, state_ref, quadrant_ref, frac_lat_ref, frac_lon_ref, land_ref,
-    out_ref, qbuf, wbuf, q_send, q_recv, w_send, w_recv, r_send, r_recv,
+    out_ref, qbuf, wbuf, wpack, whalo, q_send, q_recv, w_send, w_recv, r_send, r_recv,
     c_send, c_recv,
 ):
     n_lat, n_lon = counts
@@ -105,58 +105,53 @@
         j = pl.ds(j.start, j.stop - j.start) if isinstance(j, slice) else j
         return ref.at[i, j]
 
-    def copy(source, offset, buffer, send, recv, index):
+    def remote(source, target, way, send, recv):
+        return pltpu.make_async_remote_copy(
+            src_ref=source,
+            dst_ref=target,
+            send_sem=send,
+            recv_sem=recv,
+            device_id=peer(way),
+            device_id_type=MESH,
+        )
+
+    def q_copy(index):
         way = WAYS[index]
         si, di, _ = edge_slices(way[0], tile_lat)
         sj, dj, _ = edge_slices(way[1], tile_lon)
-
-        def moved(s):
-            return slice(s.start + offset, s.stop + offset) if isinstance(s, slice) else s + offset
-
-        return pltpu.make_async_remote_copy(
-            src_ref=at(source, moved(si), moved(sj)),
-            dst_ref=at(buffer, di, dj),
-            send_sem=send.at[index],
-            recv_sem=recv.at[index],
-            device_id=peer(way),
-            device_id_type=MESH,
+        return remote(
+            at(qx_ref, si, sj), at(qbuf, di, dj), way, q_send.at[index], q_recv.at[index]
         )
 
-    def q_copy(index):
-        return copy(qx_ref, 0, qbuf, q_send, q_recv, index)
-
-    def w_copy(index):
-        return copy(wbuf, 1, wbuf, w_send, w_recv, index)
+    def w_copy(index, part):
+        way = WAYS[2 + index]
+        source, target = (1, tile_lon + 1) if way[1] < 0 else (tile_lon, 0)
+        rows = (pl.ds(2, tile_lat - 2), pl.ds(1, 1), pl.ds(tile_lat, 1))[part]
+        return remote(
+            wbuf.at[rows, source], wbuf.at[rows, target], way,
+            w_send.at[index, part], w_recv.at[index, part],
+        )
 
     def row_copy(index, part):
-        source, target, _ = edge_slices(WAYS[index][0], tile_lat)
         width = tile_lon // row_parts
-        columns = pl.ds(1 + part * width, width)
-        return pltpu.make_async_remote_copy(
-            src_ref=wbuf.at[source + 1, columns],
-            dst_ref=wbuf.at[target, columns],
-            send_sem=r_send.at[index, part],
-            recv_sem=r_recv.at[index, part],
-            device_id=peer(WAYS[index]),
-            device_id_type=MESH,
+        return remote(
+            wpack.at[index, pl.ds(part * width, width)],
+            whalo.at[1 - index, pl.ds(1 + part * width, width)],
+            WAYS[index], r_send.at[index, part], r_recv.at[index, part],
         )
 
-    def corner_copy(buffer, stage, index):
+    def corner_copy(stage, index):
         side, step = CORNERS[index]
-        row = 0 if side < 0 else tile_lat + 1
         source, target = (1, tile_lon + 1) if step < 0 else (tile_lon, 0)
-        return pltpu.make_async_remote_copy(
-            src_ref=buffer.at[row, source],
-            dst_ref=buffer.at[row, target],
-            send_sem=c_send.at[stage, index],
-            recv_sem=c_recv.at[stage, index],
-            device_id=peer((0, step)),
-            device_id_type=MESH,
+        buffer, row = (qbuf, 0 if side < 0 else tile_lat + 1) if stage == 0 else (whalo, (side + 1) // 2)
+        return remote(
+            buffer.at[row, source], buffer.at[row, target], (0, step),
+            c_send.at[stage, index], c_recv.at[stage, index],
         )
 
-    def each_corner(buffer, stage, do):
+    def each_corner(stage, do):
         for index, way in enumerate(CORNERS):
-            where_exists(way, lambda index=index: do(corner_copy(buffer, stage, index)))
+            where_exists(way, lambda index=index: do(corner_copy(stage, index)))
 
     barrier = pltpu.get_barrier_semaphore()
     for way in WAYS:
@@ -170,12 +165,12 @@
     @pl.when(lat == 0)
     def _():
         qbuf[0] = jnp.zeros(qbuf.shape[1:], BF16)
-        wbuf[0] = jnp.zeros(wbuf.shape[1:], BF16)
+        whalo[0] = jnp.zeros(whalo.shape[1:], BF16)
 
     @pl.when(lat == n_lat - 1)
     def _():
         qbuf[tile_lat + 1] = jnp.zeros(qbuf.shape[1:], BF16)
-        wbuf[tile_lat + 1] = jnp.zeros(wbuf.shape[1:], BF16)
+        whalo[1] = jnp.zeros(whalo.shape[1:], BF16)
 
     for i in range(tile_lat):
         qbuf[i + 1, pl.ds(1, tile_lon)] = qx_ref[i]
@@ -192,7 +187,19 @@
         lax.broadcasted_iota(jnp.int32, (members, members), 0)
         == lax.broadcasted_iota(jnp.int32, (members, members), 1)
     ).astype(F32)
-    eye_b = eye.astype(BF16)
+
+    which = lax.broadcasted_iota(jnp.int32, (SIDE_ROWS, members), 0)
+    line = lax.broadcasted_iota(jnp.int32, (members // 2, members), 0)
+    lane = lax.broadcasted_iota(jnp.int32, (members // 2, members), 1)
+    upper = lane >= line
+
+    def through(row, matrix):
+        high = row.astype(BF16).astype(F32)
+        rows = jnp.where(which == 0, high, jnp.where(which == 1, row - high, 0.0))
+        return jnp.sum(nn(rows.astype(BF16), matrix), axis=0, keepdims=True)
+
+    def column(row):
+        return jnp.transpose(jnp.broadcast_to(row, (members, members)))
 
     def gram_of(i, j):
         left, right = [], []
@@ -221,7 +228,8 @@
         both = first * second
         return both, coefs, scale * both * both
 
-    def transform(places):
+    def transform(places, pack_at=None):
+        pack = pack_at is not None
         group = range(len(places))
         xs, sides, scalars = [], [], []
         for i, j in places:
@@ -260,32 +268,48 @@
                 zs[n] = d if step == 0 else (zs[n] + d) + nn(db, zs[n].astype(BF16))
             if not last:
                 xs = [(gs[n] + ds[n]) + nn(ds[n].astype(BF16), gs[n].astype(BF16)) for n in group]
-        which = lax.broadcasted_iota(jnp.int32, (SIDE_ROWS, members), 0)
         for n, (i, j) in enumerate(places):
             frob, root, _ = scalars[n]
-            side = sides[n]
             zb = zs[n].astype(BF16)
-            high = side.astype(BF16).astype(F32)
-            rows = jnp.where(which == 0, high, jnp.where(which == 1, side - high, 0.0))
-            inner = side + jnp.sum(nn(rows.astype(BF16), zb), axis=0, keepdims=True)
+            inner = sides[n] + through(sides[n], zb)
             inner = inner * (root * root / frob)
-            high = inner.astype(BF16)
-            low = (inner - high.astype(F32)).astype(BF16)
-            high = jnp.broadcast_to(high, (members, members))
-            low = jnp.broadcast_to(low, (members, members))
-            mean_weight = nt(
-                jnp.concatenate([zb, eye_b, eye_b], axis=1),
-                jnp.concatenate([high, high, low], axis=1),
-            )
+            mean_weight = inner + through(inner, zb)
             spread = math.sqrt(members - 1) * root / jnp.sqrt(frob)
-            wbuf[i + 1, j + 1] = (mean_weight + spread * (zs[n] + eye)).astype(BF16)
+            part = spread * (zs[n] + eye)
+            wbuf[i + 1, j + 1] = (part + column(mean_weight)).astype(BF16)
+            if pack:
+                half = members // 2
+                swapped = jnp.concatenate([part[half:, half:], part[half:, :half]], axis=1)
+                wpack[pack_at(n)[0], pack_at(n)[1], pl.ds(0, half), :] = jnp.where(
+                    upper, part[:half], swapped
+                ).astype(BF16)
+                diagonal = jnp.sum(part * eye, axis=0, keepdims=True)
+                high = mean_weight.astype(BF16).astype(F32)
+                wpack[pack_at(n)[0], pack_at(n)[1], pl.ds(half, SIDE_ROWS), :] = jnp.where(
+                    which == 0, diagonal,
+                    jnp.where(which == 1, high, jnp.where(which == 2, mean_weight - high, 0.0)),
+                ).astype(BF16)
+
+    def unpack(side, j):
+        half = members // 2
+        sent = whalo[side, j, pl.ds(0, half), :]
+        tail = whalo[side, j, pl.ds(half, SIDE_ROWS), :].astype(F32)
+        turned = jnp.transpose(jnp.concatenate([sent, sent], axis=0)).astype(F32)
+        sent = sent.astype(F32)
+        swapped = jnp.concatenate([sent[:, half:], sent[:, :half]], axis=1)
+        top = jnp.where(upper, sent, turned[:half])
+        low = jnp.where(lane >= half, jnp.where(lane - half < line, swapped, turned[:half]), turned[half:])
+        low = jnp.where(lane - half == line, tail[0:1], low)
+        whole = jnp.concatenate([top, low], axis=0) + column(tail[1:2] + tail[2:3])
+        wbuf[side * (tile_lat + 1), j] = whole.astype(BF16)
 
     mid_lat, mid_lon = tile_lat - 2, tile_lon - 2
     n_rows, n_sides, n_inner = 2 * tile_lon, 2 * mid_lat, mid_lat * mid_lon
     group = next(g for g in (4, 2) if all(n % g == 0 for n in (n_rows, n_sides, n_inner)))
     g_rows, g_sides, g_inner = n_rows // group, n_sides // group, n_inner // group
-    wide = next(g for g in range(16, 0, -1) if n_rows % g == 0 and mid_lat * tile_lon % g == 0)
-    w_rows, w_rest = n_rows // wide, mid_lat * tile_lon // wide
+    wide = next(g for g in range(16, 0, -1) if mid_lat * tile_lon % g == 0)
+    part_lon = tile_lon // row_parts
+    w_rest = mid_lat * tile_lon // wide
 
     def row_place(k):
         return (k % 2) * (tile_lat - 1), k // 2
@@ -296,31 +320,33 @@
     def inner_place(k):
         return 1 + k // mid_lon, 1 + k % mid_lon
 
-    def place(slot, g):
-        row = row_place(jnp.minimum(slot, w_rows - 1) * wide + g)
-        k = jnp.maximum(slot - w_rows, 0) * wide + g
-        rest = 1 + k // tile_lon, k % tile_lon
-        is_row = slot < w_rows
-        return jnp.where(is_row, row[0], rest[0]), jnp.where(is_row, row[1], rest[1])
-
-    for index in range(2):
-        received(index, q_copy)
-    each_corner(qbuf, 0, lambda copy: copy.start())
     for index in range(2, 4):
         received(index, q_copy)
-    each_corner(qbuf, 0, lambda copy: copy.wait_recv())
-
-    def node_step(slot, carry):
-        transform([place(slot, g) for g in range(wide)])
-
+
+    def rest_step(slot, carry):
+        ks = [slot * wide + g for g in range(wide)]
+        transform([(1 + k // tile_lon, k % tile_lon) for k in ks])
+        return carry
+
+    lax.fori_loop(0, w_rest, rest_step, 0)
+    for index in range(2):
+        w_copy(index, 0).start()
+    for index in range(2):
+        received(index, q_copy)
+    each_corner(0, lambda copy: copy.start())
+    each_corner(0, lambda copy: copy.wait_recv())
+
+    def row_step(part, carry):
+        spots = [(g % 2, part * part_lon + g // 2) for g in range(2 * part_lon)]
+        transform([(side * (tile_lat - 1), j) for side, j in spots], lambda n: spots[n])
         for index in range(2):
-            pl.when(exists(WAYS[index]) & (slot == w_rows - 1))(
-                lambda index=index: row_copy(index, 0).start())
-        return carry
-
-    lax.fori_loop(0, w_rows + w_rest, node_step, 0)
-    for index in range(2, 4):
-        w_copy(index).start()
+            where_exists(WAYS[index], lambda index=index: row_copy(index, part).start())
+        return carry
+
+    lax.fori_loop(0, row_parts, row_step, 0)
+    for index in range(2):
+        for part in range(1, 3):
+            w_copy(index, part).start()
 
     def analyse(i, j):
         values = state_ref[i, j].astype(F32)
@@ -359,33 +385,45 @@
     for index in range(2):
         for part in range(row_parts):
             received(index, lambda index, part=part: row_copy(index, part))
-    each_corner(wbuf, 1, lambda copy: copy.start())
-    for index in range(2, len(WAYS)):
-        received(index, w_copy)
+    each_corner(1, lambda copy: copy.start())
+    for index in range(2):
+        for part in range(3):
+            w_copy(index, part).wait_recv()
+
+    def side_step(t, carry):
+        for g in range(group):
+            analyse(*side_place(t * group + g))
+        return carry
+
+    lax.fori_loop(0, g_sides, side_step, 0)
+
+    def unpack_step(t, carry):
+        for g in range(2):
+            for side in range(2):
+                unpack(side, 1 + 2 * t + g)
+        return carry
+
+    lax.fori_loop(0, tile_lon // 2, unpack_step, 0)
+    each_corner(1, lambda copy: copy.wait_recv())
+    for side in range(2):
+        for j in (0, tile_lon + 1):
+            unpack(side, j)
 
     def rim_step(t, carry):
-        @pl.when(t == g_sides + g_rows - 2)
-        def _():
-            each_corner(wbuf, 1, lambda copy: copy.wait_recv())
-
-        part = lax.rem(t - g_sides + 1 + g_rows, g_rows)
-        first = jnp.where(t < g_sides, n_rows + t * group, part * group)
         for g in range(group):
-            k = first + g
-            row, side = row_place(jnp.minimum(k, n_rows - 1)), side_place(jnp.maximum(k - n_rows, 0))
-            analyse(jnp.where(k < n_rows, row[0], side[0]), jnp.where(k < n_rows, row[1], side[1]))
-        return carry
-
-    lax.fori_loop(0, g_rows + g_sides, rim_step, 0)
+            analyse(*row_place(t * group + g))
+        return carry
+
+    lax.fori_loop(0, g_rows, rim_step, 0)
     for index in range(len(WAYS)):
         sent(index, q_copy)
-        if index >= 2:
-            sent(index, w_copy)
-        else:
-            for part in range(row_parts):
-                sent(index, lambda index, part=part: row_copy(index, part))
-    each_corner(qbuf, 0, lambda copy: copy.wait_send())
-    each_corner(wbuf, 1, lambda copy: copy.wait_send())
+    for index in range(2):
+        for part in range(3):
+            w_copy(index, part).wait_send()
+        for part in range(row_parts):
+            sent(index, lambda index, part=part: row_copy(index, part))
+    each_corner(0, lambda copy: copy.wait_send())
+    each_corner(1, lambda copy: copy.wait_send())
 
 
 VM = pl.BlockSpec(memory_space=pltpu.VMEM)
@@ -394,7 +432,7 @@
 def body(counts, state, obs_row, obs_count, obs_value, obs_weight, quadrant, frac_lat, frac_lon, land):
     tile_lat, tile_lon, cells, members = state.shape
     rows = cells + SIDE_ROWS
-    row_parts = 1
+    row_parts = 2 if tile_lon % 2 == 0 else 1
     qx = pl.pallas_call(
         prep_kernel,
         out_shape=jax.ShapeDtypeStruct((tile_lat, tile_lon, rows, members), BF16),
@@ -410,10 +448,12 @@
         scratch_shapes=[
             pltpu.VMEM((tile_lat + 2, tile_lon + 2, rows, members), BF16),
             pltpu.VMEM((tile_lat + 2, tile_lon + 2, members, members), BF16),
+            pltpu.VMEM((2, tile_lon, members // 2 + SIDE_ROWS, members), BF16),
+            pltpu.VMEM((2, tile_lon + 2, members // 2 + SIDE_ROWS, members), BF16),
             pltpu.SemaphoreType.DMA((4,)),
             pltpu.SemaphoreType.DMA((4,)),
-            pltpu.SemaphoreType.DMA((4,)),
-            pltpu.SemaphoreType.DMA((4,)),
+            pltpu.SemaphoreType.DMA((2, 3)),
+            pltpu.SemaphoreType.DMA((2, 3)),
             pltpu.SemaphoreType.DMA((2, row_parts)),
             pltpu.SemaphoreType.DMA((2, row_parts)),
             pltpu.SemaphoreType.DMA((2, 4)),

time: 42.9 us -> 35.8 us (0.83)
  Pallas kernels: 40.6 us -> 33.7 us
    pallas_call x1, Pallas kernels: 37.4 us -> 30.5 us  [body(): pl.pallas_call(functools.partial(main_kernel, counts), out_shape=jax.Shap...]
where the time goes in v2:
time: 35.8 us; the launch traced here: 35.6 us
  Pallas kernels  33.7 us (94%)
  local copies, waits for them, and re-layouts  1.87 us (5%)
    pallas_call x1, Pallas kernels, body(): pl.pallas_call(functools.partial(main_kernel, counts), out_shape=jax.Shap...  30.5 us
    pallas_call x1, Pallas kernels, body(): pl.pallas_call(prep_kernel, out_shape=jax.ShapeDtypeStruct((tile_lat, til...  3.17 us
    unnamed x13, local copies, waits for them, and re-layouts  1.87 us

profile of v2, /device:TPU:17, one launch (start us, length us, event | category | flops | bytes accessed | tf_op | source)
XLA Modules:
  0.0 35.6 jit_solution(9191958072527128273)
XLA Ops:
  0.0 0.0 copy-start.1
  0.0 0.0 copy-start.5
  0.0 0.0 copy-start.4
  0.0 0.0 copy-start.3
  0.0 0.0 copy-start.2
  0.0 3.2 %prep.1.qx_ref = bf16[4,8,72,128]{3,2,1,0:T(8,128)(2,1)} custom-call(s32[4,8]{1,0:T(4,128)} %count_ref.1, bf16[4,8,64,128]{3,2,1,0:T(8,128)(2,1)} %state_ref.3, s32[4,8,128]{2,1,0:T(8,128)} %row_ref.1, f32[4,8,128]{2,1,0:T(8,128)} %value_ref.1, f32[4,8,128]{2,1,0:T(8,128)} %weight_ref.1), custom_call_target="tpu_custom_call" | custom-call | tf_op jit(solution)/shard_map/prep/pallas_call | solution.py:436
  3.2 0.0 copy-done.1
  3.2 0.0 copy-done.5
  3.2 0.0 copy-done.4
  3.2 0.0 copy-done.3
  3.2 0.0 copy-done.2
  3.2 0.0 copy-start
  3.2 1.1 %copy-done = bf16[4,8,72,128]{3,2,1,0:T(8,128)(2,1)S(1)} copy-done((bf16[4,8,72,128]{3,2,1,0:T(8,128)(2,1)S(1)}, bf16[4,8,72,128]{3,2,1,0:T(8,128)(2,1)}, u32[]{:S(2)}) %copy-start) | copy-done | bytes 589848
  4.3 30.5 %analyse.1 = bf16[4,8,64,128]{3,2,1,0:T(8,128)(2,1)S(1)} custom-call(bf16[4,8,72,128]{3,2,1,0:T(8,128)(2,1)S(1)} %copy-done, bf16[4,8,64,128]{3,2,1,0:T(8,128)(2,1)S(1)} %copy-done.1, s32[4,8,64]{2,1,0:T(8,128)S(1)} %copy-done.2, f32[4,8,64]{2,1,0:T(8,128)S(1)} %copy-done.3, f32[4,8,64]{2,1,0:T(8,128)S(1)} %copy-done.4, s32[4,8,64]{2,1,0:T(8,128)S(1)} %copy-done.5), custom_call_target="tpu_custom_call" | custom-call | tf_op jit(solution)/shard_map/analyse/pallas_call | solution.py:443
  34.8 0.8 %copy.11 = bf16[4,8,64,128]{3,2,1,0:T(8,128)(2,1)} copy(bf16[4,8,64,128]{3,2,1,0:T(8,128)(2,1)S(1)} %analyse.1) | data formatting | bytes 1048576
Async XLA Ops:
  0.0 3.2 %copy-start.1 = (bf16[4,8,64,128]{3,2,1,0:T(8,128)(2,1)S(1)}, bf16[4,8,64,128]{3,2,1,0:T(8,128)(2,1)}, u32[]{:S(2)}) copy-start(bf16[4,8,64,128]{3,2,1,0:T(8,128)(2,1)} %state_ref.3) | copy-start | bytes 1572868
  0.0 3.2 %copy-start.5 = (s32[4,8,64]{2,1,0:T(8,128)S(1)}, s32[4,8,64]{2,1,0:T(8,128)}, u32[]{:S(2)}) copy-start(s32[4,8,64]{2,1,0:T(8,128)} %land_ref.1) | copy-start | bytes 24580
  0.0 3.2 %copy-start.4 = (f32[4,8,64]{2,1,0:T(8,128)S(1)}, f32[4,8,64]{2,1,0:T(8,128)}, u32[]{:S(2)}) copy-start(f32[4,8,64]{2,1,0:T(8,128)} %frac_lon_ref.1) | copy-start | bytes 24580
  0.0 3.2 %copy-start.3 = (f32[4,8,64]{2,1,0:T(8,128)S(1)}, f32[4,8,64]{2,1,0:T(8,128)}, u32[]{:S(2)}) copy-start(f32[4,8,64]{2,1,0:T(8,128)} %frac_lat_ref.1) | copy-start | bytes 24580
  0.0 3.2 %copy-start.2 = (s32[4,8,64]{2,1,0:T(8,128)S(1)}, s32[4,8,64]{2,1,0:T(8,128)}, u32[]{:S(2)}) copy-start(s32[4,8,64]{2,1,0:T(8,128)} %quadrant_ref.1) | copy-start | bytes 24580
  3.2 1.1 %copy-start = (bf16[4,8,72,128]{3,2,1,0:T(8,128)(2,1)S(1)}, bf16[4,8,72,128]{3,2,1,0:T(8,128)(2,1)}, u32[]{:S(2)}) copy-start(bf16[4,8,72,128]{3,2,1,0:T(8,128)(2,1)} %prep.1.qx_ref) | copy-start | bytes 1769476

commit v3 on v2

--- a/solution.py
+++ b/solution.py
@@ -34,55 +34,36 @@
     return next(g for g in range(most, 0, -1) if count % g == 0)
 
 
-def prep_kernel(count_ref, state_ref, row_ref, value_ref, weight_ref, out_ref):
+def main_kernel(
+    counts, count_ref, state_in, row_in, value_in, weight_in, quadrant_in, frac_lat_in,
+    frac_lon_in, land_in, result,
+    state_ref, row_ref, value_ref, weight_ref, quadrant_ref, frac_lat_ref, frac_lon_ref,
+    land_ref, out_ref, qbuf, wbuf, wpack, whalo, in_sem, out_sem, q_send, q_recv, w_send,
+    w_recv, r_send, r_recv, c_send, c_recv,
+):
+    n_lat, n_lon = counts
+    row_parts = r_send.shape[2]
     tile_lat, tile_lon, cells, members = state_ref.shape
     slots = row_ref.shape[-1]
-    nodes = tile_lat * tile_lon
-    group = group_of(nodes, 8)
-
-    def step(t, carry):
-        for g in range(group):
-            node = t * group + g
-            i, j = node // tile_lon, node % tile_lon
-            values = state_ref[i, j].astype(F32)
-            mean = jnp.sum(values, axis=1, keepdims=True) * (1.0 / members)
-            pert = values - mean
-            lane = lax.broadcasted_iota(jnp.int32, (1, slots), 1)
-            weight = jnp.where(lane < count_ref[i, j], weight_ref[i, pl.ds(j, 1), :], 0.0)
-            square = weight * weight
-            hit = row_ref[i, pl.ds(j, 1), :] == lax.broadcasted_iota(jnp.int32, (cells, slots), 0)
-            density = jnp.sum(jnp.where(hit, square, 0.0), axis=1, keepdims=True)
-            pulled = jnp.sum(
-                jnp.where(hit, square * value_ref[i, pl.ds(j, 1), :], 0.0), axis=1, keepdims=True
-            )
-            out_ref[i, j, pl.ds(0, cells), :] = (jnp.sqrt(density) * pert).astype(BF16)
-            side = jnp.sum(pert * (pulled - density * mean), axis=0, keepdims=True)
-            high = side.astype(BF16).astype(F32)
-            which = lax.broadcasted_iota(jnp.int32, (SIDE_ROWS, members), 0)
-            tail = jnp.where(which == 0, high, jnp.where(which == 1, side - high, 0.0))
-            out_ref[i, j, pl.ds(cells, SIDE_ROWS), :] = tail.astype(BF16)
-        return carry
-
-    lax.fori_loop(0, nodes // group, step, 0)
-
-
-def edge_slices(step, size):
-    if step == 0:
-        return slice(0, size), slice(1, size + 1), size
-    if step < 0:
-        return 0, size + 1, 1
-    return size - 1, 0, 1
-
-
-def main_kernel(
-    counts, qx_ref, state_ref, quadrant_ref, frac_lat_ref, frac_lon_ref, land_ref,
-    out_ref, qbuf, wbuf, wpack, whalo, q_send, q_recv, w_send, w_recv, r_send, r_recv,
-    c_send, c_recv,
-):
-    n_lat, n_lon = counts
-    row_parts = r_send.shape[1]
-    tile_lat, tile_lon, cells, members = state_ref.shape
+    part_lon = tile_lon // row_parts
     lat, lon = lax.axis_index("lat"), lax.axis_index("lon")
+
+    edge_rows = (pl.ds(0, 1), pl.ds(tile_lat - 1, 1), pl.ds(1, tile_lat - 2))
+    loads = [
+        pltpu.make_async_copy(state_in.at[rows], state_ref.at[rows], in_sem.at[n])
+        for n, rows in enumerate(edge_rows)
+    ]
+    small = (
+        (row_in, row_ref), (value_in, value_ref), (weight_in, weight_ref),
+        (quadrant_in, quadrant_ref), (frac_lat_in, frac_lat_ref),
+        (frac_lon_in, frac_lon_ref), (land_in, land_ref),
+    )
+    loads += [
+        pltpu.make_async_copy(source, target, in_sem.at[3 + n])
+        for n, (source, target) in enumerate(small)
+    ]
+    for n in (3, 4, 5, 0, 1, 2, 6, 7, 8, 9):
+        loads[n].start()
 
     def exists(way):
         if way[0] < 0:
@@ -99,11 +80,6 @@
 
     def peer(way):
         return (lat + way[0], lax.rem(lon + way[1] + n_lon, n_lon))
-
-    def at(ref, i, j):
-        i = pl.ds(i.start, i.stop - i.start) if isinstance(i, slice) else i
-        j = pl.ds(j.start, j.stop - j.start) if isinstance(j, slice) else j
-        return ref.at[i, j]
 
     def remote(source, target, way, send, recv):
         return pltpu.make_async_remote_copy(
@@ -115,12 +91,26 @@
             device_id_type=MESH,
         )
 
-    def q_copy(index):
-        way = WAYS[index]
-        si, di, _ = edge_slices(way[0], tile_lat)
-        sj, dj, _ = edge_slices(way[1], tile_lon)
+    def column_of(part, t):
+        if row_parts == 1:
+            return t
+        quarter = part_lon // 2
+        return jnp.where(part == 0, quarter + t, t if t < quarter else t + part_lon)
+
+    def q_lon(index):
+        source, target = ((1, tile_lon + 1), (tile_lon, 0))[index]
+        rows = pl.ds(1, tile_lat)
         return remote(
-            at(qx_ref, si, sj), at(qbuf, di, dj), way, q_send.at[index], q_recv.at[index]
+            qbuf.at[rows, source], qbuf.at[rows, target], WAYS[2 + index],
+            q_send.at[index], q_recv.at[index],
+        )
+
+    def q_row(index, part):
+        source, target = ((1, tile_lat + 1), (tile_lat, 0))[index]
+        columns = pl.ds(1 + part * part_lon, part_lon)
+        return remote(
+            qbuf.at[source, columns], qbuf.at[target, columns], WAYS[index],
+            r_send.at[0, index, part], r_recv.at[0, index, part],
         )
 
     def w_copy(index, part):
@@ -133,20 +123,25 @@
         )
 
     def row_copy(index, part):
-        width = tile_lon // row_parts
+        columns = pl.ds(part * part_lon, part_lon)
         return remote(
-            wpack.at[index, pl.ds(part * width, width)],
-            whalo.at[1 - index, pl.ds(1 + part * width, width)],
-            WAYS[index], r_send.at[index, part], r_recv.at[index, part],
+            wpack.at[index, columns], whalo.at[1 - index, columns],
+            WAYS[index], r_send.at[1, index, part], r_recv.at[1, index, part],
         )
 
     def corner_copy(stage, index):
         side, step = CORNERS[index]
-        source, target = (1, tile_lon + 1) if step < 0 else (tile_lon, 0)
-        buffer, row = (qbuf, 0 if side < 0 else tile_lat + 1) if stage == 0 else (whalo, (side + 1) // 2)
+        if stage == 0:
+            row = 0 if side < 0 else tile_lat + 1
+            source, target = (1, tile_lon + 1) if step < 0 else (tile_lon, 0)
+            source, target = qbuf.at[row, source], qbuf.at[row, target]
+        else:
+            row = 0 if side < 0 else 1
+            first = part_lon if row_parts == 2 else 0
+            source, target = (first, tile_lon + 1) if step < 0 else (tile_lon - 1, tile_lon)
+            source, target = whalo.at[row, source], whalo.at[row, target]
         return remote(
-            buffer.at[row, source], buffer.at[row, target], (0, step),
-            c_send.at[stage, index], c_recv.at[stage, index],
+            source, target, (0, step), c_send.at[stage, index], c_recv.at[stage, index]
         )
 
     def each_corner(stage, do):
@@ -158,10 +153,6 @@
         where_exists(way, lambda way=way: pl.semaphore_signal(
             barrier, inc=1, device_id=peer(way), device_id_type=MESH))
     present = 2 + (lat > 0).astype(jnp.int32) + (lat < n_lat - 1).astype(jnp.int32)
-    pl.semaphore_wait(barrier, present)
-    for index, way in enumerate(WAYS):
-        where_exists(way, lambda index=index: q_copy(index).start())
-
     @pl.when(lat == 0)
     def _():
         qbuf[0] = jnp.zeros(qbuf.shape[1:], BF16)
@@ -172,9 +163,6 @@
         qbuf[tile_lat + 1] = jnp.zeros(qbuf.shape[1:], BF16)
         whalo[1] = jnp.zeros(whalo.shape[1:], BF16)
 
-    for i in range(tile_lat):
-        qbuf[i + 1, pl.ds(1, tile_lon)] = qx_ref[i]
-
     def received(index, make):
         way = WAYS[index]
         back = (-way[0], -way[1])
@@ -183,12 +171,36 @@
     def sent(index, make):
         where_exists(WAYS[index], lambda: make(index).wait_send())
 
+    which = lax.broadcasted_iota(jnp.int32, (SIDE_ROWS, members), 0)
+    flat = jnp.full((members, members), 1.0 / members, BF16)
+
+    def prepare(i, j):
+        values = state_ref[i, j]
+        mean = nn(values, flat)
+        pert = values.astype(F32) - mean
+        spot = lax.broadcasted_iota(jnp.int32, (1, slots), 1)
+        weight = jnp.where(spot < count_ref[i, j], weight_ref[i, pl.ds(j, 1), :], 0.0)
+        square = weight * weight
+        hit = row_ref[i, pl.ds(j, 1), :] == lax.broadcasted_iota(jnp.int32, (cells, slots), 0)
+        hit = jnp.where(hit, 1.0, 0.0).astype(BF16)
+        wide = []
+        for row in (square, square * value_ref[i, pl.ds(j, 1), :]):
+            high = row.astype(BF16).astype(F32)
+            both = jnp.concatenate([high, row - high], axis=1)
+            wide.append(jnp.broadcast_to(both, (members, 2 * slots)).astype(BF16))
+        sums = nt(jnp.concatenate([hit, hit], axis=1), jnp.concatenate(wide, axis=0))
+        density, pulled = sums[:, :members], sums[:, members:]
+        qbuf[i + 1, j + 1, pl.ds(0, cells), :] = (jnp.sqrt(density) * pert).astype(BF16)
+        side = jnp.sum(pert * (pulled - density * mean), axis=0, keepdims=True)
+        high = side.astype(BF16).astype(F32)
+        tail = jnp.where(which == 0, high, jnp.where(which == 1, side - high, 0.0))
+        qbuf[i + 1, j + 1, pl.ds(cells, SIDE_ROWS), :] = tail.astype(BF16)
+
     eye = (
         lax.broadcasted_iota(jnp.int32, (members, members), 0)
         == lax.broadcasted_iota(jnp.int32, (members, members), 1)
     ).astype(F32)
 
-    which = lax.broadcasted_iota(jnp.int32, (SIDE_ROWS, members), 0)
     line = lax.broadcasted_iota(jnp.int32, (members // 2, members), 0)
     lane = lax.broadcasted_iota(jnp.int32, (members // 2, members), 1)
     upper = lane >= line
@@ -290,10 +302,10 @@
                     jnp.where(which == 1, high, jnp.where(which == 2, mean_weight - high, 0.0)),
                 ).astype(BF16)
 
-    def unpack(side, j):
+    def unpack(side, spot, j):
         half = members // 2
-        sent = whalo[side, j, pl.ds(0, half), :]
-        tail = whalo[side, j, pl.ds(half, SIDE_ROWS), :].astype(F32)
+        sent = whalo[side, spot, pl.ds(0, half), :]
+        tail = whalo[side, spot, pl.ds(half, SIDE_ROWS), :].astype(F32)
         turned = jnp.transpose(jnp.concatenate([sent, sent], axis=0)).astype(F32)
         sent = sent.astype(F32)
         swapped = jnp.concatenate([sent[:, half:], sent[:, :half]], axis=1)
@@ -308,8 +320,8 @@
     group = next(g for g in (4, 2) if all(n % g == 0 for n in (n_rows, n_sides, n_inner)))
     g_rows, g_sides, g_inner = n_rows // group, n_sides // group, n_inner // group
     wide = next(g for g in range(16, 0, -1) if mid_lat * tile_lon % g == 0)
-    part_lon = tile_lon // row_parts
     w_rest = mid_lat * tile_lon // wide
+    ready = next(g for g in range(8, 0, -1) if mid_lat * tile_lon % g == 0)
 
     def row_place(k):
         return (k % 2) * (tile_lat - 1), k // 2
@@ -320,8 +332,35 @@
     def inner_place(k):
         return 1 + k // mid_lon, 1 + k % mid_lon
 
-    for index in range(2, 4):
-        received(index, q_copy)
+    for n in (3, 4, 5, 0, 1):
+        loads[n].wait()
+
+    def first_step(t, carry):
+        for g in range(2 * part_lon):
+            prepare((g % 2) * (tile_lat - 1), t * part_lon + g // 2)
+
+        @pl.when(t == 0)
+        def _():
+            pl.semaphore_wait(barrier, present)
+
+        for index in range(2):
+            where_exists(WAYS[index], lambda index=index: q_row(index, t).start())
+        return carry
+
+    lax.fori_loop(0, row_parts, first_step, 0)
+    loads[2].wait()
+
+    def ready_step(t, carry):
+        for g in range(ready):
+            k = t * ready + g
+            prepare(1 + k // tile_lon, k % tile_lon)
+        return carry
+
+    lax.fori_loop(0, mid_lat * tile_lon // ready, ready_step, 0)
+    for index in range(2):
+        q_lon(index).start()
+    for index in range(2):
+        q_lon(index).wait_recv()
 
     def rest_step(slot, carry):
         ks = [slot * wide + g for g in range(wide)]
@@ -332,13 +371,20 @@
     for index in range(2):
         w_copy(index, 0).start()
     for index in range(2):
-        received(index, q_copy)
+        for part in range(row_parts):
+            received(index, lambda index, part=part: q_row(index, part))
     each_corner(0, lambda copy: copy.start())
-    each_corner(0, lambda copy: copy.wait_recv())
 
     def row_step(part, carry):
-        spots = [(g % 2, part * part_lon + g // 2) for g in range(2 * part_lon)]
-        transform([(side * (tile_lat - 1), j) for side, j in spots], lambda n: spots[n])
+        @pl.when(part == row_parts - 1)
+        def _():
+            each_corner(0, lambda copy: copy.wait_recv())
+
+        spots = [(g % 2, g // 2) for g in range(2 * part_lon)]
+        transform(
+            [(side * (tile_lat - 1), column_of(part, t)) for side, t in spots],
+            lambda n: (spots[n][0], part * part_lon + spots[n][1]),
+        )
         for index in range(2):
             where_exists(WAYS[index], lambda index=index: row_copy(index, part).start())
         return carry
@@ -349,8 +395,9 @@
             w_copy(index, part).start()
 
     def analyse(i, j):
-        values = state_ref[i, j].astype(F32)
-        mean = jnp.sum(values, axis=1, keepdims=True) * (1.0 / members)
+        values = state_ref[i, j]
+        mean = nn(values, flat)
+        values = values.astype(F32)
         pert = (values - mean).astype(BF16)
         corner = quadrant_ref[i, pl.ds(j, 1), :]
         along = []
@@ -376,12 +423,32 @@
         result = jnp.where(coef[:, 6:7] == 1.0, acc, values)
         out_ref[i, j] = result.astype(BF16)
 
-    def inner_step(t, carry):
-        for g in range(group):
-            analyse(*inner_place(t * group + g))
-        return carry
-
-    lax.fori_loop(0, g_inner, inner_step, 0)
+    for n in range(6, 10):
+        loads[n].wait()
+    middle = pl.ds(1, mid_lat)
+    stores = [
+        pltpu.make_async_copy(out_ref.at[rows, columns], result.at[rows, columns], out_sem.at[n])
+        for n, (rows, columns) in enumerate((
+            (middle, pl.ds(1, mid_lon)), (middle, pl.ds(0, 1)), (middle, pl.ds(tile_lon - 1, 1)),
+            (pl.ds(0, 1), pl.ds(1, mid_lon)), (pl.ds(tile_lat - 1, 1), pl.ds(1, mid_lon)),
+            (pl.ds(0, 1), pl.ds(0, 1)), (pl.ds(0, 1), pl.ds(tile_lon - 1, 1)),
+            (pl.ds(tile_lat - 1, 1), pl.ds(0, 1)),
+            (pl.ds(tile_lat - 1, 1), pl.ds(tile_lon - 1, 1)),
+        ))
+    ]
+
+    def analyse_all(count, place):
+        each = next(g for g in range(4, 0, -1) if count % g == 0)
+
+        def step(t, carry):
+            for g in range(each):
+                analyse(*place(t * each + g))
+            return carry
+
+        lax.fori_loop(0, count // each, step, 0)
+
+    analyse_all(n_inner, inner_place)
+    stores[0].start()
     for index in range(2):
         for part in range(row_parts):
             received(index, lambda index, part=part: row_copy(index, part))
@@ -389,81 +456,77 @@
     for index in range(2):
         for part in range(3):
             w_copy(index, part).wait_recv()
-
-    def side_step(t, carry):
-        for g in range(group):
-            analyse(*side_place(t * group + g))
+    analyse_all(n_sides, side_place)
+    stores[1].start()
+    stores[2].start()
+
+    def unpack_step(part, carry):
+        for t in range(part_lon):
+            for side in range(2):
+                unpack(side, part * part_lon + t, 1 + column_of(part, t))
         return carry
 
-    lax.fori_loop(0, g_sides, side_step, 0)
-
-    def unpack_step(t, carry):
-        for g in range(2):
-            for side in range(2):
-                unpack(side, 1 + 2 * t + g)
-        return carry
-
-    lax.fori_loop(0, tile_lon // 2, unpack_step, 0)
+    lax.fori_loop(0, row_parts, unpack_step, 0)
+    analyse_all(n_rows - 4, lambda k: row_place(k + 2))
+    stores[3].start()
+    stores[4].start()
     each_corner(1, lambda copy: copy.wait_recv())
     for side in range(2):
-        for j in (0, tile_lon + 1):
-            unpack(side, j)
-
-    def rim_step(t, carry):
-        for g in range(group):
-            analyse(*row_place(t * group + g))
-        return carry
-
-    lax.fori_loop(0, g_rows, rim_step, 0)
-    for index in range(len(WAYS)):
-        sent(index, q_copy)
-    for index in range(2):
+        for n in range(2):
+            unpack(side, tile_lon + n, n * (tile_lon + 1))
+    analyse_all(4, lambda k: ((k % 2) * (tile_lat - 1), (k // 2) * (tile_lon - 1)))
+    for n in range(5, 9):
+        stores[n].start()
+    for store in stores:
+        store.wait()
+    for index in range(2):
+        q_lon(index).wait_send()
         for part in range(3):
             w_copy(index, part).wait_send()
         for part in range(row_parts):
+            sent(index, lambda index, part=part: q_row(index, part))
             sent(index, lambda index, part=part: row_copy(index, part))
     each_corner(0, lambda copy: copy.wait_send())
     each_corner(1, lambda copy: copy.wait_send())
 
 
-VM = pl.BlockSpec(memory_space=pltpu.VMEM)
+ANY = pl.BlockSpec(memory_space=pltpu.HBM)
 
 
 def body(counts, state, obs_row, obs_count, obs_value, obs_weight, quadrant, frac_lat, frac_lon, land):
     tile_lat, tile_lon, cells, members = state.shape
     rows = cells + SIDE_ROWS
-    row_parts = 2 if tile_lon % 2 == 0 else 1
-    qx = pl.pallas_call(
-        prep_kernel,
-        out_shape=jax.ShapeDtypeStruct((tile_lat, tile_lon, rows, members), BF16),
-        in_specs=[pl.BlockSpec(memory_space=pltpu.SMEM)] + [VM] * 4,
-        out_specs=VM,
-        name="prep",
-    )(obs_count, state, obs_row, obs_value, obs_weight)
+    row_parts = 2 if tile_lon % 4 == 0 else 1
+    packed = members // 2 + SIDE_ROWS
+    arrays = (state, obs_row, obs_value, obs_weight, quadrant, frac_lat, frac_lon, land)
+    dma = pltpu.SemaphoreType.DMA
     return pl.pallas_call(
         functools.partial(main_kernel, counts),
         out_shape=jax.ShapeDtypeStruct(state.shape, BF16),
-        in_specs=[VM] * 6,
-        out_specs=VM,
-        scratch_shapes=[
+        in_specs=[pl.BlockSpec(memory_space=pltpu.SMEM)] + [ANY] * len(arrays),
+        out_specs=ANY,
+        scratch_shapes=[pltpu.VMEM(x.shape, x.dtype) for x in arrays] + [
+            pltpu.VMEM(state.shape, BF16),
             pltpu.VMEM((tile_lat + 2, tile_lon + 2, rows, members), BF16),
             pltpu.VMEM((tile_lat + 2, tile_lon + 2, members, members), BF16),
-            pltpu.VMEM((2, tile_lon, members // 2 + SIDE_ROWS, members), BF16),
-            pltpu.VMEM((2, tile_lon + 2, members // 2 + SIDE_ROWS, members), BF16),
-            pltpu.SemaphoreType.DMA((4,)),
-            pltpu.SemaphoreType.DMA((4,)),
-            pltpu.SemaphoreType.DMA((2, 3)),
-            pltpu.SemaphoreType.DMA((2, 3)),
-            pltpu.SemaphoreType.DMA((2, row_parts)),
-            pltpu.SemaphoreType.DMA((2, row_parts)),
-            pltpu.SemaphoreType.DMA((2, 4)),
-            pltpu.SemaphoreType.DMA((2, 4)),
+            pltpu.VMEM((2, tile_lon, packed, members), BF16),
+            pltpu.VMEM((2, tile_lon + 2, packed, members), BF16),
+            dma((10,)),
+            dma((9,)),
+            dma((2,)),
+            dma((2,)),
+            dma((2, 3)),
+            dma((2, 3)),
+            dma((2, 2, row_parts)),
+            dma((2, 2, row_parts)),
+            dma((2, 4)),
+            dma((2, 4)),
         ],
         compiler_params=pltpu.CompilerParams(
-            collective_id=0, has_side_effects=True, vmem_limit_bytes=48 * 1024 * 1024
+            collective_id=0, has_side_effects=True, vmem_limit_bytes=63 * 1024 * 1024
         ),
         name="analyse",
-    )(qx, state, quadrant, frac_lat, frac_lon, land)
+    )(obs_count, *arrays)
 
 
 def solution(mesh):

time: 35.8 us -> 32.9 us (0.919)
  Pallas kernels: 33.7 us -> 30.8 us
    pallas_call x1 -> x0, Pallas kernels: 3.17 us -> none  [body(): pl.pallas_call(prep_kernel, out_shape=jax.ShapeDtypeStruct((tile_lat, til...]
    unnamed x13 -> x1, local copies, waits for them, and re-layouts: 1.87 us -> 1.87 us
where the time goes in v3:
time: 32.9 us; the launch traced here: 32.6 us
  Pallas kernels  30.8 us (94%)
  local copies, waits for them, and re-layouts  1.87 us (6%)
    pallas_call x1, Pallas kernels, body(): pl.pallas_call(functools.partial(main_kernel, counts), out_shape=jax.Shap...  30.8 us
    unnamed x1, local copies, waits for them, and re-layouts  1.87 us

profile of v3, /device:TPU:17, one launch (start us, length us, event | category | flops | bytes accessed | tf_op | source)
XLA Modules:
  0.0 32.6 jit_solution(8881491836094837676)
XLA Ops:
  0.0 30.8 %analyse.1 = bf16[4,8,64,128]{3,2,1,0:T(8,128)(2,1)} custom-call(s32[4,8]{1,0:T(4,128)} %count_ref.1, bf16[4,8,64,128]{3,2,1,0:T(8,128)(2,1)} %state_in.1, s32[4,8,128]{2,1,0:T(8,128)} %row_in.1, f32[4,8,128]{2,1,0:T(8,128)} %value_in.1, f32[4,8,128]{2,1,0:T(8,128)} %weight_in.1, s32[4,8,64]{2,1,0:T(8,128)} %quadrant_in.1, f32[4,8,64]{2,1,0:T(8,128)} %frac_lat_in.1, ...), custom_call_target="tpu_custom_call" | custom-call | tf_op jit(solution)/shard_map/analyse/pallas_call | solution.py:503
  30.8 1.9 %copy.11 = bf16[4,8,64,128]{3,2,1,0:T(8,128)(2,1)} copy(bf16[4,8,64,128]{3,2,1,0:T(8,128)(2,1)} %analyse.1) | data formatting | bytes 1048576

commit v4 on v3

--- a/solution.py
+++ b/solution.py
@@ -35,10 +35,10 @@
 
 
 def main_kernel(
-    counts, count_ref, state_in, row_in, value_in, weight_in, quadrant_in, frac_lat_in,
-    frac_lon_in, land_in, result,
-    state_ref, row_ref, value_ref, weight_ref, quadrant_ref, frac_lat_ref, frac_lon_ref,
-    land_ref, out_ref, qbuf, wbuf, wpack, whalo, in_sem, out_sem, q_send, q_recv, w_send,
+    counts, count_in, state_in, row_in, value_in, weight_in, quadrant_in, frac_lat_in,
+    frac_lon_in, land_in, out_ref,
+    count_ref, state_ref, row_ref, value_ref, weight_ref, quadrant_ref, frac_lat_ref, frac_lon_ref,
+    land_ref, qbuf, wbuf, wpack, whalo, in_sem, q_send, q_recv, w_send,
     w_recv, r_send, r_recv, c_send, c_recv,
 ):
     n_lat, n_lon = counts
@@ -57,12 +57,13 @@
         (row_in, row_ref), (value_in, value_ref), (weight_in, weight_ref),
         (quadrant_in, quadrant_ref), (frac_lat_in, frac_lat_ref),
         (frac_lon_in, frac_lon_ref), (land_in, land_ref),
+        (count_in, count_ref),
     )
     loads += [
         pltpu.make_async_copy(source, target, in_sem.at[3 + n])
         for n, (source, target) in enumerate(small)
     ]
-    for n in (3, 4, 5, 0, 1, 2, 6, 7, 8, 9):
+    for n in (10, 3, 4, 5, 0, 1, 2, 6, 7, 8, 9):
         loads[n].start()
 
     def exists(way):
@@ -332,7 +333,7 @@
     def inner_place(k):
         return 1 + k // mid_lon, 1 + k % mid_lon
 
-    for n in (3, 4, 5, 0, 1):
+    for n in (10, 3, 4, 5, 0, 1):
         loads[n].wait()
 
     def first_step(t, carry):
@@ -400,45 +401,35 @@
         values = values.astype(F32)
         pert = (values - mean).astype(BF16)
         corner = quadrant_ref[i, pl.ds(j, 1), :]
+        kept = land_ref[i, pl.ds(j, 1), :] != 1
         along = []
         for half, frac in (
             (corner // 2, frac_lat_ref[i, pl.ds(j, 1), :]),
             (corner % 2, frac_lon_ref[i, pl.ds(j, 1), :]),
         ):
-            for a in range(3):
-                along.append(
-                    jnp.where(half == a, 1.0 - frac, 0.0) + jnp.where(half + 1 == a, frac, 0.0)
-                )
-        along.append(land_ref[i, pl.ds(j, 1), :].astype(F32))
-        along.append(jnp.zeros_like(along[0]))
+            along.append(jnp.where(half == 0, 1.0 - frac, 0.0))
+            along.append(jnp.where(half == 1, frac, 0.0))
+        along[0] = jnp.where(kept, 2.0, along[0])
+        along += [jnp.zeros_like(along[1])] * 4
         coef = jnp.transpose(jnp.concatenate(along, axis=0))
+        edges = [jnp.broadcast_to(coef[:, n : n + 1], (cells, members)) for n in range(4)]
+        kept = edges[0] > 1.5
+        spread_lat = (edges[0], 1.0 - edges[0] - edges[1], edges[1])
+        spread_lon = (edges[2], 1.0 - edges[2] - edges[3], edges[3])
         acc = mean
         for a in range(3):
             wide = jnp.concatenate([wbuf[i + a, j + b] for b in range(3)], axis=1)
             prod = nn(pert, wide)
             row = sum(
-                coef[:, 3 + b : 4 + b] * prod[:, b * members : (b + 1) * members] for b in range(3)
+                spread_lon[b] * prod[:, b * members : (b + 1) * members] for b in range(3)
             )
-            acc = acc + coef[:, a : a + 1] * row
-        result = jnp.where(coef[:, 6:7] == 1.0, acc, values)
-        out_ref[i, j] = result.astype(BF16)
+            acc = acc + spread_lat[a] * row
+        out_ref[i, j] = jnp.where(kept, values, acc).astype(BF16)
 
     for n in range(6, 10):
         loads[n].wait()
-    middle = pl.ds(1, mid_lat)
-    stores = [
-        pltpu.make_async_copy(out_ref.at[rows, columns], result.at[rows, columns], out_sem.at[n])
-        for n, (rows, columns) in enumerate((
-            (middle, pl.ds(1, mid_lon)), (middle, pl.ds(0, 1)), (middle, pl.ds(tile_lon - 1, 1)),
-            (pl.ds(0, 1), pl.ds(1, mid_lon)), (pl.ds(tile_lat - 1, 1), pl.ds(1, mid_lon)),
-            (pl.ds(0, 1), pl.ds(0, 1)), (pl.ds(0, 1), pl.ds(tile_lon - 1, 1)),
-            (pl.ds(tile_lat - 1, 1), pl.ds(0, 1)),
-            (pl.ds(tile_lat - 1, 1), pl.ds(tile_lon - 1, 1)),
-        ))
-    ]
-
     def analyse_all(count, place):
-        each = next(g for g in range(4, 0, -1) if count % g == 0)
+        each = next(g for g in range(12, 0, -1) if count % g == 0)
 
         def step(t, carry):
             for g in range(each):
@@ -448,7 +439,6 @@
         lax.fori_loop(0, count // each, step, 0)
 
     analyse_all(n_inner, inner_place)
-    stores[0].start()
     for index in range(2):
         for part in range(row_parts):
             received(index, lambda index, part=part: row_copy(index, part))
@@ -457,8 +447,6 @@
         for part in range(3):
             w_copy(index, part).wait_recv()
     analyse_all(n_sides, side_place)
-    stores[1].start()
-    stores[2].start()
 
     def unpack_step(part, carry):
         for t in range(part_lon):
@@ -468,17 +456,11 @@
 
     lax.fori_loop(0, row_parts, unpack_step, 0)
     analyse_all(n_rows - 4, lambda k: row_place(k + 2))
-    stores[3].start()
-    stores[4].start()
     each_corner(1, lambda copy: copy.wait_recv())
     for side in range(2):
         for n in range(2):
             unpack(side, tile_lon + n, n * (tile_lon + 1))
     analyse_all(4, lambda k: ((k % 2) * (tile_lat - 1), (k // 2) * (tile_lon - 1)))
-    for n in range(5, 9):
-        stores[n].start()
-    for store in stores:
-        store.wait()
     for index in range(2):
         q_lon(index).wait_send()
         for part in range(3):
@@ -498,21 +480,22 @@
     rows = cells + SIDE_ROWS
     row_parts = 2 if tile_lon % 4 == 0 else 1
     packed = members // 2 + SIDE_ROWS
+    hbm = pltpu.HBM
     arrays = (state, obs_row, obs_value, obs_weight, quadrant, frac_lat, frac_lon, land)
     dma = pltpu.SemaphoreType.DMA
     return pl.pallas_call(
         functools.partial(main_kernel, counts),
         out_shape=jax.ShapeDtypeStruct(state.shape, BF16),
-        in_specs=[pl.BlockSpec(memory_space=pltpu.SMEM)] + [ANY] * len(arrays),
-        out_specs=ANY,
-        scratch_shapes=[pltpu.VMEM(x.shape, x.dtype) for x in arrays] + [
-            pltpu.VMEM(state.shape, BF16),
+        in_specs=[ANY] * (1 + len(arrays)),
+        out_specs=pl.BlockSpec(memory_space=pltpu.VMEM),
+        scratch_shapes=[pltpu.SMEM(obs_count.shape, obs_count.dtype)]
+        + [pltpu.VMEM(x.shape, x.dtype) for x in arrays]
+        + [
             pltpu.VMEM((tile_lat + 2, tile_lon + 2, rows, members), BF16),
             pltpu.VMEM((tile_lat + 2, tile_lon + 2, members, members), BF16),
             pltpu.VMEM((2, tile_lon, packed, members), BF16),
             pltpu.VMEM((2, tile_lon + 2, packed, members), BF16),
-            dma((10,)),
-            dma((9,)),
+            dma((11,)),
             dma((2,)),
             dma((2,)),
             dma((2, 3)),
@@ -523,10 +506,10 @@
             dma((2, 4)),
         ],
         compiler_params=pltpu.CompilerParams(
-            collective_id=0, has_side_effects=True, vmem_limit_bytes=63 * 1024 * 1024
+            collective_id=0, has_side_effects=True, vmem_limit_bytes=48 * 1024 * 1024
         ),
         name="analyse",
-    )(obs_count, *arrays)
+    )(*(pltpu.with_memory_space_constraint(x, hbm) for x in (obs_count, *arrays)))
 
 
 def solution(mesh):

time: 32.9 us -> 30 us (0.912)
  Pallas kernels: 30.8 us -> 29 us
  local copies, waits for them, and re-layouts: 1.87 us -> 0.8 us
    pallas_call x1, Pallas kernels: 30.8 us -> 29 us  [body(): pl.pallas_call(functools.partial(main_kernel, counts), out_shape=jax.Shap...]
    unnamed x1, local copies, waits for them, and re-layouts: 1.87 us -> 0.8 us
where the time goes in v4:
time: 30 us; the launch traced here: 29.8 us
  Pallas kernels  29 us (97%)
  local copies, waits for them, and re-layouts  0.8 us (3%)
    pallas_call x1, Pallas kernels, body(): pl.pallas_call(functools.partial(main_kernel, counts), out_shape=jax.Shap...  29 us
    unnamed x1, local copies, waits for them, and re-layouts  0.8 us

profile of v4, /device:TPU:17, one launch (start us, length us, event | category | flops | bytes accessed | tf_op | source)
XLA Modules:
  0.0 29.8 jit_solution(1154881573910774635)
XLA Ops:
  0.0 29.0 %analyse.1 = bf16[4,8,64,128]{3,2,1,0:T(8,128)(2,1)S(1)} custom-call(s32[4,8]{1,0:T(4,128)} %count_in.1, bf16[4,8,64,128]{3,2,1,0:T(8,128)(2,1)} %state_in.1, s32[4,8,128]{2,1,0:T(8,128)} %row_in.1, f32[4,8,128]{2,1,0:T(8,128)} %value_in.1, f32[4,8,128]{2,1,0:T(8,128)} %weight_in.1, s32[4,8,64]{2,1,0:T(8,128)} %quadrant_in.1, f32[4,8,64]{2,1,0:T(8,128)} %frac_lat_in.1, ...), custom_call_target="tpu_custom_call" | custom-call | tf_op jit(solution)/shard_map/analyse/pallas_call | solution.py:486
  29.0 0.8 %copy.11 = bf16[4,8,64,128]{3,2,1,0:T(8,128)(2,1)} copy(bf16[4,8,64,128]{3,2,1,0:T(8,128)(2,1)S(1)} %analyse.1) | data formatting | bytes 1048576

commit v5 on v4

--- a/solution.py
+++ b/solution.py
@@ -38,7 +38,7 @@
     counts, count_in, state_in, row_in, value_in, weight_in, quadrant_in, frac_lat_in,
     frac_lon_in, land_in, out_ref,
     count_ref, state_ref, row_ref, value_ref, weight_ref, quadrant_ref, frac_lat_ref, frac_lon_ref,
-    land_ref, qbuf, wbuf, wpack, whalo, in_sem, q_send, q_recv, w_send,
+    land_ref, acc_ref, share_ref, pert_ref, qbuf, wbuf, wpack, whalo, in_sem, q_send, q_recv, w_send,
     w_recv, r_send, r_recv, c_send, c_recv,
 ):
     n_lat, n_lon = counts
@@ -395,7 +395,7 @@
         for part in range(1, 3):
             w_copy(index, part).start()
 
-    def analyse(i, j):
+    def analyse(i, j, side=None):
         values = state_ref[i, j]
         mean = nn(values, flat)
         values = values.astype(F32)
@@ -416,15 +416,35 @@
         kept = edges[0] > 1.5
         spread_lat = (edges[0], 1.0 - edges[0] - edges[1], edges[1])
         spread_lon = (edges[2], 1.0 - edges[2] - edges[3], edges[3])
+        halo = None if side is None else 2 * side
         acc = mean
         for a in range(3):
+            if a == halo:
+                continue
             wide = jnp.concatenate([wbuf[i + a, j + b] for b in range(3)], axis=1)
             prod = nn(pert, wide)
             row = sum(
                 spread_lon[b] * prod[:, b * members : (b + 1) * members] for b in range(3)
             )
             acc = acc + spread_lat[a] * row
-        out_ref[i, j] = jnp.where(kept, values, acc).astype(BF16)
+        acc = jnp.where(kept, values, acc)
+        if side is None:
+            out_ref[i, j] = acc.astype(BF16)
+        else:
+            share = jnp.where(kept, 0.0, spread_lat[halo])
+            acc_ref[side, j] = acc
+            pert_ref[side, j] = pert
+            for b in range(3):
+                share_ref[side, j, b] = share * spread_lon[b]
+
+    def finish(side, j):
+        i = side * (tile_lat - 1)
+        wide = jnp.concatenate([wbuf[side * (tile_lat + 1), j + b] for b in range(3)], axis=1)
+        prod = nn(pert_ref[side, j], wide)
+        acc = acc_ref[side, j]
+        for b in range(3):
+            acc = acc + share_ref[side, j, b] * prod[:, b * members : (b + 1) * members]
+        out_ref[i, j] = acc.astype(BF16)
 
     for n in range(6, 10):
         loads[n].wait()
@@ -440,12 +460,21 @@
 
     analyse_all(n_inner, inner_place)
     for index in range(2):
+        for part in range(3):
+            w_copy(index, part).wait_recv()
+    each_own = next(g for g in (4, 2, 1) if tile_lon % g == 0)
+
+    def own_step(t, carry):
+        for g in range(each_own):
+            for side in range(2):
+                analyse(side * (tile_lat - 1), t * each_own + g, side)
+        return carry
+
+    lax.fori_loop(0, tile_lon // each_own, own_step, 0)
+    for index in range(2):
         for part in range(row_parts):
             received(index, lambda index, part=part: row_copy(index, part))
     each_corner(1, lambda copy: copy.start())
-    for index in range(2):
-        for part in range(3):
-            w_copy(index, part).wait_recv()
     analyse_all(n_sides, side_place)
 
     def unpack_step(part, carry):
@@ -455,12 +484,16 @@
         return carry
 
     lax.fori_loop(0, row_parts, unpack_step, 0)
-    analyse_all(n_rows - 4, lambda k: row_place(k + 2))
+    for j in range(1, tile_lon - 1):
+        for side in range(2):
+            finish(side, j)
     each_corner(1, lambda copy: copy.wait_recv())
     for side in range(2):
         for n in range(2):
             unpack(side, tile_lon + n, n * (tile_lon + 1))
-    analyse_all(4, lambda k: ((k % 2) * (tile_lat - 1), (k // 2) * (tile_lon - 1)))
+    for j in (0, tile_lon - 1):
+        for side in range(2):
+            finish(side, j)
     for index in range(2):
         q_lon(index).wait_send()
         for part in range(3):
@@ -491,6 +524,9 @@
         scratch_shapes=[pltpu.SMEM(obs_count.shape, obs_count.dtype)]
         + [pltpu.VMEM(x.shape, x.dtype) for x in arrays]
         + [
+            pltpu.VMEM((2, tile_lon, cells, members), F32),
+            pltpu.VMEM((2, tile_lon, 3, cells, members), F32),
+            pltpu.VMEM((2, tile_lon, cells, members), BF16),
             pltpu.VMEM((tile_lat + 2, tile_lon + 2, rows, members), BF16),
             pltpu.VMEM((tile_lat + 2, tile_lon + 2, members, members), BF16),
             pltpu.VMEM((2, tile_lon, packed, members), BF16),

time: 30 us -> 29.1 us (0.970)
  Pallas kernels: 29 us -> 28 us
    pallas_call x1, Pallas kernels: 29 us -> 28 us  [body(): pl.pallas_call(functools.partial(main_kernel, counts), out_shape=jax.Shap...]
where the time goes in v5:
time: 29.1 us; the launch traced here: 28.8 us
  Pallas kernels  28 us (96%)
  local copies, waits for them, and re-layouts  0.8 us (3%)
    pallas_call x1, Pallas kernels, body(): pl.pallas_call(functools.partial(main_kernel, counts), out_shape=jax.Shap...  28 us
    unnamed x1, local copies, waits for them, and re-layouts  0.8 us

profile of v5, /device:TPU:17, one launch (start us, length us, event | category | flops | bytes accessed | tf_op | source)
XLA Modules:
  0.0 28.8 jit_solution(3259303094077895940)
XLA Ops:
  0.0 28.0 %analyse.1 = bf16[4,8,64,128]{3,2,1,0:T(8,128)(2,1)S(1)} custom-call(s32[4,8]{1,0:T(4,128)} %count_in.1, bf16[4,8,64,128]{3,2,1,0:T(8,128)(2,1)} %state_in.1, s32[4,8,128]{2,1,0:T(8,128)} %row_in.1, f32[4,8,128]{2,1,0:T(8,128)} %value_in.1, f32[4,8,128]{2,1,0:T(8,128)} %weight_in.1, s32[4,8,64]{2,1,0:T(8,128)} %quadrant_in.1, f32[4,8,64]{2,1,0:T(8,128)} %frac_lat_in.1, ...), custom_call_target="tpu_custom_call" | custom-call | tf_op jit(solution)/shard_map/analyse/pallas_call | solution.py:519
  28.0 0.8 %copy.11 = bf16[4,8,64,128]{3,2,1,0:T(8,128)(2,1)} copy(bf16[4,8,64,128]{3,2,1,0:T(8,128)(2,1)S(1)} %analyse.1) | data formatting | bytes 1048576

commit v6 on v5

--- a/solution.py
+++ b/solution.py
@@ -354,12 +354,17 @@
     def ready_step(t, carry):
         for g in range(ready):
             k = t * ready + g
-            prepare(1 + k // tile_lon, k % tile_lon)
+            p = k // mid_lat
+            prepare(1 + k % mid_lat, jnp.where(p % 2 == 0, p // 2, tile_lon - 1 - p // 2))
+
+        @pl.when(t == (2 * mid_lat + ready - 1) // ready - 1)
+        def _():
+            for index in range(2):
+                q_lon(index).start()
+
         return carry
 
     lax.fori_loop(0, mid_lat * tile_lon // ready, ready_step, 0)
-    for index in range(2):
-        q_lon(index).start()
     for index in range(2):
         q_lon(index).wait_recv()
 
@@ -471,19 +476,22 @@
         return carry
 
     lax.fori_loop(0, tile_lon // each_own, own_step, 0)
-    for index in range(2):
-        for part in range(row_parts):
-            received(index, lambda index, part=part: row_copy(index, part))
-    each_corner(1, lambda copy: copy.start())
-    analyse_all(n_sides, side_place)
 
     def unpack_step(part, carry):
+        for index in range(2):
+            received(index, lambda index: row_copy(index, part))
+
+        @pl.when(part == row_parts - 1)
+        def _():
+            each_corner(1, lambda copy: copy.start())
+
         for t in range(part_lon):
             for side in range(2):
                 unpack(side, part * part_lon + t, 1 + column_of(part, t))
         return carry
 
     lax.fori_loop(0, row_parts, unpack_step, 0)
+    analyse_all(n_sides, side_place)
     for j in range(1, tile_lon - 1):
         for side in range(2):
             finish(side, j)

time: 29.1 us -> 28.9 us (level)
  no operation moved by 1% of the time
where the time goes in v6:
time: 28.9 us; the launch traced here: 28.7 us
  Pallas kernels  27.9 us (97%)
  local copies, waits for them, and re-layouts  0.8 us (3%)
    pallas_call x1, Pallas kernels, body(): pl.pallas_call(functools.partial(main_kernel, counts), out_shape=jax.Shap...  27.9 us
    unnamed x1, local copies, waits for them, and re-layouts  0.8 us

profile of v6, /device:TPU:17, one launch (start us, length us, event | category | flops | bytes accessed | tf_op | source)
XLA Modules:
  0.0 28.7 jit_solution(15377355325444473356)
XLA Ops:
  0.0 27.9 %analyse.1 = bf16[4,8,64,128]{3,2,1,0:T(8,128)(2,1)S(1)} custom-call(s32[4,8]{1,0:T(4,128)} %count_in.1, bf16[4,8,64,128]{3,2,1,0:T(8,128)(2,1)} %state_in.1, s32[4,8,128]{2,1,0:T(8,128)} %row_in.1, f32[4,8,128]{2,1,0:T(8,128)} %value_in.1, f32[4,8,128]{2,1,0:T(8,128)} %weight_in.1, s32[4,8,64]{2,1,0:T(8,128)} %quadrant_in.1, f32[4,8,64]{2,1,0:T(8,128)} %frac_lat_in.1, ...), custom_call_target="tpu_custom_call" | custom-call | tf_op jit(solution)/shard_map/analyse/pallas_call | solution.py:527
  27.9 0.8 %copy.11 = bf16[4,8,64,128]{3,2,1,0:T(8,128)(2,1)} copy(bf16[4,8,64,128]{3,2,1,0:T(8,128)(2,1)S(1)} %analyse.1) | data formatting | bytes 1048576
